TPU v7x, 128 devices: a whole 4x4x4 slice. The times are simulated.
128 devices in a mesh: context: 16 (over y, x), head: 4 (over z), doc: 2 (over core).
Axes of the slice: x: 4, y: 4, z: 4, core: 2. Of those that a mesh axis runs over, the one named last changes fastest.
Arguments:
- x_input: bfloat16 [16384, 8192], P(('doc', 'context'), 'head'), parts along dimension 0, may hold values from -6 to 6
- b_input: bfloat16 [16384, 1024], P(('doc', 'context'), 'head'), parts along dimension 0, may hold values from -6 to 6
- c_input: bfloat16 [16384, 1024], P(('doc', 'context'), 'head'), parts along dimension 0, may hold values from -6 to 6
- kernel_x: float32 [4, 8192], P(None, 'head'), may hold values from -3 to 3
- kernel_b: float32 [4, 1024], P(None, 'head'), may hold values from -3 to 3
- kernel_c: float32 [4, 1024], P(None, 'head'), may hold values from -3 to 3
- step_size: float32 [16384, 128], P(('doc', 'context'), 'head'), parts along dimension 0, may hold values from 1.2207031e-05 to 0.3, as said below
- decay_log: float32 [128], P('head'), may hold values from 0 to 0.69
- skip_gain: float32 [128], P('head'), may hold values from 0.1 to 1.9
- grad_output: bfloat16 [16384, 8192], P(('doc', 'context'), 'head'), parts along dimension 0, may hold values from -6 to 6
Outputs:
- layer_output: bfloat16 [16384, 8192], P(('doc', 'context'), 'head'), parts along dimension 0
- grad_x: bfloat16 [16384, 8192], P(('doc', 'context'), 'head'), parts along dimension 0
- grad_b: bfloat16 [16384, 1024], P(('doc', 'context'), 'head'), parts along dimension 0
- grad_c: bfloat16 [16384, 1024], P(('doc', 'context'), 'head'), parts along dimension 0
There are 2 independent parts, one for each index of `doc`. A program takes and returns all parts, laid end to end along the dimension named above; an argument that names none is the same for every part. Nothing has to cross between parts.
Inputs may be any that keep to these rules, and one draw needn't show every extreme that they name: `step_size`: positive step sizes.
All inputs are finite; a program needn't handle non-finite values.
Results may differ from a plain program's by a relative error of at most 0.018.
Values may be sent and summed in bfloat16 or wider, within the bound.
A program may use at most 256 MiB of HBM per device.

v0:
```python
import jax
import jax.numpy as jnp
from jax import lax
from jax.sharding import PartitionSpec as P

SPACE_HEADS = 128
HEAD_DIM = 64
STATE = 256
GROUPS = 4
BLOCK = 128


def from_behind(array, axis, by):
    peers = lax.axis_size(axis)
    pairs = [(i, i + by) for i in range(peers) if 0 <= i + by < peers]
    return lax.ppermute(array, axis, pairs)


def entering(array, axis, join, neutral, backward):
    count = lax.axis_size(axis)
    place = lax.axis_index(axis)
    ahead = count - 1 - place if backward else place
    gathered = jax.tree.map(
        lambda a, kind: lax.all_gather(a.astype(kind), axis), array, (jnp.bfloat16, jnp.bfloat16)
    )
    state = jax.tree.map(lambda a, e: jnp.zeros_like(a) + jnp.asarray(e, a.dtype), array, neutral)

    def one(turn, state):
        source = count - 1 - turn if backward else turn
        return join(
            state,
            jax.tree.map(
                lambda a, own: lax.dynamic_index_in_dim(a, source, 0, False).astype(own.dtype),
                gathered,
                array,
            ),
        )

    return lax.fori_loop(0, ahead, one, state)


def product(form, left, right):
    return jnp.einsum(form, left, right, preferred_element_type=jnp.float32)


def silu_slope(pre_act):
    sigmoid = jax.nn.sigmoid(pre_act)
    return sigmoid * (1.0 + pre_act * (1.0 - sigmoid))


def decay_table(cumulative):
    transposed = jnp.transpose(cumulative, (0, 2, 3, 1))
    differ = transposed[..., :, None] - transposed[..., None, :]
    positions = jnp.arange(cumulative.shape[1])
    lower_mask = positions[:, None] >= positions[None, :]
    return jnp.where(lower_mask, jnp.exp(jnp.minimum(differ, 0.0)), 0.0)


def conv_apply(padded, kernel, length):
    result = jnp.zeros((length, padded.shape[1]), jnp.float32)
    for offset in range(kernel.shape[0]):
        result = result + kernel[offset][None, :] * padded[offset : offset + length].astype(
            jnp.float32
        )
    return result


def conv_back(padded_grad, kernel, length):
    result = jnp.zeros((length, padded_grad.shape[1]), jnp.float32)
    width_k = kernel.shape[0]
    for offset in range(width_k):
        begin = width_k - 1 - offset
        result = result + kernel[offset][None, :] * padded_grad[begin : begin + length].astype(
            jnp.float32
        )
    return result


def chain_forward(block_state, block_total, initial):

    def advance(carried, pair_in):
        state_k, total_k = pair_in
        return (jnp.exp(total_k)[..., None, None] * carried + state_k, carried)

    return lax.scan(advance, initial, (block_state, block_total))


def chain_backward(block_adj, block_total, initial):

    def retreat(carried, pair_in):
        adj_k, total_k = pair_in
        return (jnp.exp(total_k)[..., None, None] * carried + adj_k, carried)

    return lax.scan(retreat, initial, (block_adj, block_total), reverse=True)


def combine_chain(earlier, later):
    return (earlier[0] + later[0], jnp.exp(later[0])[..., None, None] * earlier[1] + later[1])


def prepare(blk_x, blk_b, blk_c, step_block, log_block, grad_block):
    cumulative = jnp.cumsum(log_block, axis=1)
    table = decay_table(cumulative)
    scores = product("nigs,njgs->ngij", blk_c, blk_b)
    mixing = (table * scores[:, :, None]).astype(jnp.bfloat16)
    scaled_x = (blk_x * step_block[..., None]).astype(jnp.bfloat16)
    block_total = cumulative[:, -1]
    to_end = jnp.exp(block_total[:, None] - cumulative)
    weighted_x = (scaled_x * to_end[..., None]).astype(jnp.bfloat16)
    block_state = product("njgap,njgs->ngaps", weighted_x, blk_b)
    growth = jnp.exp(cumulative)
    grad_weighted = (grad_block * growth[..., None]).astype(jnp.bfloat16)
    block_adj = product("nigap,nigs->ngaps", grad_weighted, blk_c)
    return (
        table,
        mixing,
        scaled_x,
        to_end,
        weighted_x,
        growth,
        grad_weighted,
        block_total,
        block_state,
        block_adj,
    )


def finish(prepared, blk_x, blk_b, blk_c, step_block, skip_block, grad_block, starts, afters):
    table, mixing, scaled_x, to_end, weighted_x, growth, grad_weighted = prepared[:7]
    start_bf = starts.astype(jnp.bfloat16)
    after_bf = afters.astype(jnp.bfloat16)
    intra_part = product("ngaij,njgap->nigap", mixing, scaled_x)
    carried_in = growth[..., None] * product("nigs,ngaps->nigap", blk_c, start_bf)
    output = (intra_part + carried_in + skip_block[:, :, None] * blk_x.astype(jnp.float32)).astype(
        jnp.bfloat16
    )
    inner_grad = product("ngaij,nigap->njgap", mixing, grad_block)
    outer_grad = to_end[..., None] * product("njgs,ngaps->njgap", blk_b, after_bf)
    grad_act_x = step_block[..., None] * (inner_grad + outer_grad) + skip_block[
        :, :, None
    ] * grad_block.astype(jnp.float32)
    pair_sum = jnp.sum(table * product("nigap,njgap->ngaij", grad_block, scaled_x), axis=2).astype(
        jnp.bfloat16
    )
    grad_act_b = product("ngij,nigs->njgs", pair_sum, blk_c) + product(
        "njgap,ngaps->njgs", weighted_x, after_bf
    )
    grad_act_c = product("ngij,njgs->nigs", pair_sum, blk_b) + product(
        "nigap,ngaps->nigs", grad_weighted, start_bf
    )
    return (output, grad_act_x, grad_act_b, grad_act_c)


def on_device(
    x_input,
    b_input,
    c_input,
    kernel_x,
    kernel_b,
    kernel_c,
    step_size,
    decay_log,
    skip_gain,
    grad_output,
):
    length = x_input.shape[0]
    margin = kernel_x.shape[0] - 1
    prior_x, prior_b, prior_c = from_behind(
        (x_input[length - margin :], b_input[length - margin :], c_input[length - margin :]),
        "context",
        1,
    )
    padded_x = jnp.concatenate([prior_x, x_input], axis=0)
    padded_b = jnp.concatenate([prior_b, b_input], axis=0)
    padded_c = jnp.concatenate([prior_c, c_input], axis=0)
    pre_x = conv_apply(padded_x, kernel_x, length)
    pre_b = conv_apply(padded_b, kernel_b, length)
    pre_c = conv_apply(padded_c, kernel_c, length)
    act_x = jax.nn.silu(pre_x).astype(jnp.bfloat16)
    act_b = jax.nn.silu(pre_b).astype(jnp.bfloat16)
    act_c = jax.nn.silu(pre_c).astype(jnp.bfloat16)
    groups_dev = b_input.shape[1] // STATE
    per_group = SPACE_HEADS // GROUPS
    blocks = length // BLOCK
    log_step = step_size * (-jnp.exp(decay_log))[None, :]
    shape_x = (blocks, BLOCK, groups_dev, per_group, HEAD_DIM)
    shape_h = (blocks, BLOCK, groups_dev, per_group)
    shape_b = (blocks, BLOCK, groups_dev, STATE)
    blk_x = act_x.reshape(shape_x)
    blk_b = act_b.reshape(shape_b)
    blk_c = act_c.reshape(shape_b)
    step_block = step_size.reshape(shape_h)
    log_block = log_step.reshape(shape_h)
    grad_block = grad_output.reshape(shape_x)
    skip_block = skip_gain.reshape(groups_dev, per_group)
    prepared = prepare(blk_x, blk_b, blk_c, step_block, log_block, grad_block)
    block_total, block_state, block_adj = (prepared[7], prepared[8], prepared[9])
    empty = jnp.zeros(block_state.shape[1:], jnp.float32)
    device_total = jnp.sum(block_total, axis=0)
    local_end, local_starts = chain_forward(block_state, block_total, empty)
    local_first, local_afters = chain_backward(block_adj, block_total, empty)
    identity = (jnp.zeros(device_total.shape, jnp.float32), empty)
    state_pair = entering((device_total, local_end), "context", combine_chain, identity, False)
    adjoint_pair = entering((device_total, local_first), "context", combine_chain, identity, True)
    state_in = state_pair[1]
    adjoint_in = adjoint_pair[1]
    starts = chain_forward(block_state, block_total, state_in)[1]
    afters = chain_backward(block_adj, block_total, adjoint_in)[1]
    output, grad_act_x, grad_act_b, grad_act_c = finish(
        prepared, blk_x, blk_b, blk_c, step_block, skip_block, grad_block, starts, afters
    )
    grad_pre_x = (grad_act_x.reshape(length, -1) * silu_slope(pre_x)).astype(jnp.bfloat16)
    grad_pre_b = (grad_act_b.reshape(length, -1) * silu_slope(pre_b)).astype(jnp.bfloat16)
    grad_pre_c = (grad_act_c.reshape(length, -1) * silu_slope(pre_c)).astype(jnp.bfloat16)
    next_x, next_b, next_c = from_behind(
        (grad_pre_x[:margin], grad_pre_b[:margin], grad_pre_c[:margin]), "context", -1
    )
    grad_x = conv_back(jnp.concatenate([grad_pre_x, next_x], axis=0), kernel_x, length).astype(
        jnp.bfloat16
    )
    grad_b = conv_back(jnp.concatenate([grad_pre_b, next_b], axis=0), kernel_b, length).astype(
        jnp.bfloat16
    )
    grad_c = conv_back(jnp.concatenate([grad_pre_c, next_c], axis=0), kernel_c, length).astype(
        jnp.bfloat16
    )
    return (output.reshape(length, -1), grad_x, grad_b, grad_c)


def solution(mesh):
    return jax.shard_map(
        on_device,
        mesh=mesh,
        in_specs=(
            P(("doc", "context"), "head"),
            P(("doc", "context"), "head"),
            P(("doc", "context"), "head"),
            P(None, "head"),
            P(None, "head"),
            P(None, "head"),
            P(("doc", "context"), "head"),
            P("head"),
            P("head"),
            P(("doc", "context"), "head"),
        ),
        out_specs=(
            P(("doc", "context"), "head"),
            P(("doc", "context"), "head"),
            P(("doc", "context"), "head"),
            P(("doc", "context"), "head"),
        ),
        check_vma=False,
    )
```

profile of v0, /device:TPU:2, one launch (start us, length us, event | category | flops | bytes accessed | tf_op | source)
XLA Modules:
  0.0 455.5 jit_solution(10980666134170681163)
XLA Ops:
  23.9 3.9 copy.128
  29.6 11.2 %fusion.27 = (f32[512,2048]{0,1:T(8,128)}, f32[512,2048]{0,1:T(8,128)}) fusion(bf16[512,2048]{0,1:T(8,128)(2,1)} %copy.128, f32[2048]{0:T(1024)} %bitcast.241, bf16[3,2048]{0,1:T(8,128)(2,1)} %collective-permute-done, f32[2048]{0:T(1024)} %bitcast.243, f32[2048]{0:T(1024)S(1)} %bitcast.239, f32[2048]{0:T(1024)S(1)} %bitcast.237), kind=kLoop, calls=%fused_computation.67 | loop fusion | flops 27262976 | bytes 10530816 | tf_op jit(solution)/shard_map/convert_element_type | solution.py:106
  40.7 5.2 %reshape.337 = f32[4,128,32,64]{1,0,3,2:T(4,128)} reshape(f32[512,2048]{0,1:T(8,128)} %get-tuple-element.586) | data formatting | bytes 8388608 | tf_op jit(solution)/shard_map/convert_element_type | solution.py:106
  48.8 4.5 convolution_bitcast_fusion.1
  53.4 10.4 %while.84 = (s32[]{:T(128)}, f32[1,32,64,256]{3,2,1,0:T(8,128)S(1)}, f32[4,1,32]{2,1,0:T(1,128)}, f32[4,1,32,64,256]{4,3,2,1,0:T(8,128)}, s32[]{:T(128)}, /*index=5*/s32[]{:T(128)}) while((s32[]{:T(128)}, f32[1,32,64,256]{3,2,1,0:T(8,128)S(1)}, f32[4,1,32]{2,1,0:T(1,128)}, f32[4,1,32,64,256]{4,3,2,1,0:T(8,128)}, s32[]{:T(128)}, ...), condition=%wide.region_3.4_spmd.clone, body=%wide.region_2.3_spmd.clone.sunk | while | flops 1572867 | bytes 6291935 | solution.py:85
  65.6 3.4 collective-permute-start.1
  69.1 3.9 copy.147
  73.0 4.1 reshape.330
  78.7 36.9 %all-reduce = bf16[512]{0:T(512)(128)(2,1)S(1)} all-reduce(bf16[512]{0:T(512)(128)(2,1)S(1)} %dynamic-update-slice), channel_id=2, replica_groups=mesh['context'=16,'head'=4,'doc'=2] {'context'}, use_global_device_ids=true, to_apply=%add | all-reduce | flops 512 | bytes 2048
  116.5 4.4 multiply_convert_fusion.1
  121.0 4.4 fusion.4
  125.4 52.9 %all-gather.6.cloned.1.call-done = bf16[16,32,64,256]{3,2,1,0:T(8,128)(2,1)} async-done(((bf16[1,32,64,256]{3,2,1,0:T(8,128)(2,1)}), bf16[16,32,64,256]{3,2,1,0:T(8,128)(2,1)}) %all-gather.6.cloned.1.call-update) | async-done | bytes 16777232 | tf_op jit(solution)/shard_map/all_gather | solution.py:24
  182.9 15.2 %while.81 = (s32[]{:T(128)}, f32[1,32,64,256]{3,2,1,0:T(8,128)S(1)}, bf16[4,1,32,64,256]{4,3,2,1,0:T(8,128)(2,1)}, f32[4,1,32]{2,1,0:T(1,128)}, f32[4,1,32,64,256]{4,3,2,1,0:T(8,128)}, /*index=5*/s32[]{:T(128)}) while((s32[]{:T(128)}, f32[1,32,64,256]{3,2,1,0:T(8,128)S(1)}, bf16[4,1,32,64,256]{4,3,2,1,0:T(8,128)(2,1)}, f32[4,1,32]{2,1,0:T(1,128)}, ...), condition=%wide.region_7.8_spmd, body=%wide.region_6.7_spmd.sunk | while | flops 1048578 | bytes 10486233 | solution.py:85
  198.2 3.9 fusion.36
  204.4 4.5 convolution_bitcast_fusion
  209.0 12.4 %while.85 = (s32[]{:T(128)}, f32[1,32,64,256]{3,2,1,0:T(8,128)S(1)}, f32[4,1,32]{2,1,0:T(1,128)}, f32[4,1,32,64,256]{4,3,2,1,0:T(8,128)}, s32[]{:T(128)}, /*index=5*/s32[]{:T(128)}, s32[]{:T(128)}) while((s32[]{:T(128)}, f32[1,32,64,256]{3,2,1,0:T(8,128)S(1)}, f32[4,1,32]{2,1,0:T(1,128)}, f32[4,1,32,64,256]{4,3,2,1,0:T(8,128)}, ...), condition=%wide.region_9.10_spmd.clone, body=%wide.region_8.9_spmd.clone.sunk | while | flops 1572868 | bytes 6291955 | solution.py:94
  222.5 7.4 %reshape.353 = f32[4,128,1,32,64]{4,3,1,0,2:T(8,128)} reshape(bf16[512,2048]{1,0:T(8,128)(2,1)} %param.31) | data formatting | bytes 6291456 | tf_op jit(solution)/shard_map/convert_element_type | solution.py:112
  230.0 8.0 %copy.159 = f32[4,128,1,32,64]{1,4,3,0,2:T(8,128)} copy(f32[4,128,1,32,64]{4,3,1,0,2:T(8,128)} %reshape.353) | data formatting | bytes 8388608 | tf_op jit(solution)/shard_map/convert_element_type | solution.py:112
  237.9 5.3 %reshape.338 = f32[4,128,1,32,64]{1,0,4,3,2:T(4,128)} reshape(f32[512,2048]{0,1:T(8,128)} %get-tuple-element.586) | data formatting | bytes 8388608 | tf_op jit(solution)/shard_map/convert_element_type | solution.py:106
  246.0 3.6 fusion.18
  250.1 3.6 fusion.11
  254.8 6.4 %copy.175 = bf16[4,128,1,32,64]{4,3,1,0,2:T(8,128)(2,1)} copy(bf16[4,128,1,32,64]{1,4,3,0,2:T(8,128)(2,1)S(1)} %fusion.11) | data formatting | bytes 4194304
  261.1 6.8 %reshape.352 = bf16[512,2048]{1,0:T(8,128)(2,1)} reshape(bf16[4,128,1,32,64]{4,3,1,0,2:T(8,128)(2,1)} %copy.175) | data formatting | bytes 4194304
  269.7 86.4 %all-gather.8.cloned.1.call-done = bf16[16,32,64,256]{3,2,1,0:T(8,128)(2,1)} async-done(((bf16[1,32,64,256]{3,2,1,0:T(8,128)(2,1)}), bf16[16,32,64,256]{3,2,1,0:T(8,128)(2,1)}) %all-gather.8.cloned.1.call-update) | async-done | bytes 16777232 | tf_op jit(solution)/shard_map/all_gather | solution.py:24
  356.3 32.4 %while.82 = (s32[]{:T(128)}, f32[1,32,64,256]{3,2,1,0:T(8,128)S(1)}, s32[]{:T(128)}, bf16[16,1,32]{2,1,0:T(2,128)(2,1)}, bf16[16,1,32,64,256]{4,3,2,1,0:T(8,128)...) while((s32[]{:T(128)}, f32[1,32,64,256]{3,2,1,0:T(8,128)S(1)}, s32[]{:T(128)}, ...), condition=%wide.region_11.12_spmd, body=%wide.region_10.11_spmd.sunk | while | flops 1572902 | bytes 5243355 | solution.py:39
  391.3 15.2 %while.83 = (s32[]{:T(128)}, f32[1,32,64,256]{3,2,1,0:T(8,128)S(1)}, bf16[4,1,32,64,256]{4,3,2,1,0:T(8,128)(2,1)}, f32[4,1,32]{2,1,0:T(1,128)}, f32[4,1,32,64,256]{4,3,2,1,0:T(8,128)}, /*index=5*/s32[]{:T(128)}, s32[]{:T(128)}) while((s32[]{:T(128)}, f32[1,32,64,256]{3,2,1,0:T(8,128)S(1)}, bf16[4,1,32,64,256]{4,3,2,1,0:T(8,128)(2,1)}, ...), condition=%wide.region_13.14_spmd, body=%wide.region_12.13_spmd.sunk | while | flops 1048579 | bytes 10486253 | solution.py:94
  406.5 3.6 fusion.14
  410.6 3.7 fusion.8
  414.3 3.7 copy.160
  419.2 4.9 %collective-permute-start.4 = (bf16[3,256]{1,0:T(4,128)(2,1)S(1)}, bf16[3,256]{1,0:T(4,128)(2,1)S(1)}, u32[]{:S(2)}, u32[]{:S(2)}) collective-permute-start(bf16[3,256]{1,0:T(4,128)(2,1)S(1)} %slice.178), channel_id=1, source_target_pairs={{8,0},{16,8},{24,16},{32,24},{40,32},{48,40},{56,48},{64,56},{72,6... | collective-permute-start | bytes 4616 | tf_op jit(solution)/shard_map/ppermute | solution.py:16
  428.8 12.2 %collective-permute-done.3 = bf16[3,2048]{0,1:T(8,128)(2,1)S(1)} collective-permute-done((bf16[3,2048]{0,1:T(8,128)(2,1)S(1)}, bf16[3,2048]{0,1:T(8,128)(2,1)S(1)}, u32[]{:S(2)}, u32[]{:S(2)}) %collective-permute-start.3) | collective-permute-done | bytes 12320 | tf_op jit(solution)/shard_map/ppermute | solution.py:16
  441.0 5.2 %add_convert_fusion = bf16[512,2048]{0,1:T(8,128)(2,1)S(1)} fusion(bf16[512,2048]{0,1:T(8,128)(2,1)S(1)} %fusion.5, bf16[3,2048]{0,1:T(8,128)(2,1)S(1)} %collective-permute-done.3, f32[2048]{0:T(1024)S(1)} %bitcast.242, f32[2048]{0:T(1024)S(1)} %bitcast.244, f32[2048]{0:T(1024)S(1)} %bitcast.240, f32[2048]{0:T(1024)S(1)} %bitcast.238), kind=kLoop, calls=%fused_computation.45 | loop fusion | flops 22020096 | bytes 4239360 | tf_op jit(solution)/shard_map/convert_element_type | solution.py:218
  (232 shorter events, 136.4 us)
Async XLA Ops:
  7.2 21.2 %copy-start.15 = (bf16[512,256]{1,0:T(8,128)(2,1)S(1)}, bf16[512,256]{1,0:T(8,128)(2,1)}, u32[]{:S(2)}) copy-start(bf16[512,256]{1,0:T(8,128)(2,1)} %param.23) | copy-start | bytes 786436
  7.2 171.1 %all-gather.6.cloned.1.call-start = ((), (), s32[]{:S(2)}) async-start(), calls=%async_computation | async-start | bytes 17825792 | tf_op jit(solution)/shard_map/all_gather | solution.py:24
  7.9 19.9 %collective-permute-start.2 = (bf16[3,256]{1,0:T(4,128)(2,1)S(1)}, bf16[3,256]{1,0:T(4,128)(2,1)S(1)}, u32[]{:S(2)}, u32[]{:S(2)}) collective-permute-start(bf16[3,256]{1,0:T(4,128)(2,1)S(1)} %slice.140), channel_id=1, source_target_pairs={{0,8},{8,16},{16,24},{24,32},{32,40},{40,48},{48,56},{56,64},{64,7... | collective-permute-start | bytes 4616 | tf_op jit(solution)/shard_map/ppermute | solution.py:16
  13.2 16.4 %collective-permute-start = (bf16[3,2048]{0,1:T(8,128)(2,1)}, bf16[3,2048]{0,1:T(8,128)(2,1)}, u32[]{:S(2)}, u32[]{:S(2)}) collective-permute-start(bf16[3,2048]{0,1:T(8,128)(2,1)} %copy.127), channel_id=1, source_target_pairs={{0,8},{8,16},{16,24},{24,32},{32,40},{40,48},{48,56},{56,64},{64,7... | collective-permute-start | bytes 36872 | tf_op jit(solution)/shard_map/ppermute | solution.py:16
  20.3 25.7 %copy-start.17 = (f32[4,128,32]{1,2,0:T(8,128)}, f32[4,128,32]{1,2,0:T(8,128)S(1)}, u32[]{:S(2)}) copy-start(f32[4,128,32]{1,2,0:T(8,128)S(1)} %copy_bitcast_fusion) | copy-start | bytes 196612
  22.5 26.4 %copy-start.13 = (f32[4,128,32]{1,2,0:T(8,128)}, f32[4,128,32]{1,2,0:T(8,128)S(1)}, u32[]{:S(2)}) copy-start(f32[4,128,32]{1,2,0:T(8,128)S(1)} %get-tuple-element.593) | copy-start | bytes 196612
  64.9 291.2 %all-gather.8.cloned.1.call-start = ((), (), s32[]{:S(2)}) async-start(), calls=%async_computation.1 | async-start | bytes 17825792 | tf_op jit(solution)/shard_map/all_gather | solution.py:24
  65.6 136.8 %collective-permute-start.1 = (bf16[3,256]{1,0:T(4,128)(2,1)S(1)}, bf16[3,256]{1,0:T(4,128)(2,1)S(1)}, u32[]{:S(2)}, u32[]{:S(2)}) collective-permute-start(bf16[3,256]{1,0:T(4,128)(2,1)S(1)} %slice.132), channel_id=1, source_target_pairs={{0,8},{8,16},{16,24},{24,32},{32,40},{40,48},{48,56},{56,64},{64,7... | collective-permute-start | bytes 4616 | tf_op jit(solution)/shard_map/ppermute | solution.py:16
  69.0 8.1 %copy-start.21 = (f32[4,128,32]{1,2,0:T(8,128)S(1)}, f32[4,128,32]{1,2,0:T(8,128)}, u32[]{:S(2)}) copy-start(f32[4,128,32]{1,2,0:T(8,128)} %get-tuple-element.594) | copy-start | bytes 196612
  69.0 8.2 %copy-start.50 = (u32[128]{0:T(128)S(1)}, u32[128]{0:T(128)}, u32[]{:S(2)}) copy-start(u32[128]{0:T(128)} %constant.165) | copy-start | bytes 1540
  69.1 9.4 %copy-start.47 = (bf16[32]{0:T(256)(128)(2,1)S(1)}, bf16[32]{0:T(256)(128)(2,1)}, u32[]{:S(2)}) copy-start(bf16[32]{0:T(256)(128)(2,1)} %get-tuple-element.591) | copy-start | bytes 196
  69.1 46.8 %copy-start.44 = (f32[4,256]{1,0:T(4,128)S(1)}, f32[4,256]{1,0:T(4,128)}, u32[]{:S(2)}) copy-start(f32[4,256]{1,0:T(4,128)} %param.27) | copy-start | bytes 12292
  73.0 47.9 %copy-start.5 = (bf16[4,128,32,64]{1,3,2,0:T(8,128)(2,1)S(1)}, bf16[4,128,32,64]{1,3,2,0:T(8,128)(2,1)}, u32[]{:S(2)}) copy-start(bf16[4,128,32,64]{1,3,2,0:T(8,128)(2,1)} %copy-done.4) | copy-start | bytes 6291460
  115.8 9.5 %copy-start.25 = (f32[4,32,128]{2,1,0:T(8,128)}, f32[4,32,128]{2,1,0:T(8,128)S(1)}, u32[]{:S(2)}) copy-start(f32[4,32,128]{2,1,0:T(8,128)S(1)} %copy.133) | copy-start | bytes 196612
  115.8 5.1 %copy-start.8 = (bf16[4,128,32,64]{1,0,3,2:T(4,128)(2,1)S(1)}, bf16[4,128,32,64]{1,0,3,2:T(4,128)(2,1)}, u32[]{:S(2)}) copy-start(bf16[4,128,32,64]{1,0,3,2:T(4,128)(2,1)} %reshape.330) | copy-start | bytes 6291460
  115.9 9.5 %copy-start.28 = (pred[128,128]{0,1:T(8,128)(4,1)}, pred[128,128]{0,1:T(8,128)(4,1)S(1)}, u32[]{:S(2)}) copy-start(pred[128,128]{0,1:T(8,128)(4,1)S(1)} %iota_compare_fusion) | copy-start | bytes 49156
  198.1 4.9 %copy-start.16 = (bf16[512,256]{1,0:T(8,128)(2,1)S(1)}, bf16[512,256]{1,0:T(8,128)(2,1)}, u32[]{:S(2)}) copy-start(bf16[512,256]{1,0:T(8,128)(2,1)} %param.24) | copy-start | bytes 786436
  198.1 4.9 %copy-start.31 = (f32[1,256]{1,0:T(1,128)S(1)}, f32[1,256]{1,0:T(1,128)}, u32[]{:S(2)}) copy-start(f32[1,256]{1,0:T(1,128)} %get-tuple-element.599) | copy-start | bytes 3076
  198.1 4.9 %copy-start.33 = (f32[1,256]{1,0:T(1,128)S(1)}, f32[1,256]{1,0:T(1,128)}, u32[]{:S(2)}) copy-start(f32[1,256]{1,0:T(1,128)} %get-tuple-element.600) | copy-start | bytes 3076
  198.2 4.9 %copy-start.35 = (f32[1,256]{1,0:T(1,128)S(1)}, f32[1,256]{1,0:T(1,128)}, u32[]{:S(2)}) copy-start(f32[1,256]{1,0:T(1,128)} %get-tuple-element.601) | copy-start | bytes 3076
  198.2 4.9 %copy-start.37 = (f32[1,256]{1,0:T(1,128)S(1)}, f32[1,256]{1,0:T(1,128)}, u32[]{:S(2)}) copy-start(f32[1,256]{1,0:T(1,128)} %get-tuple-element.602) | copy-start | bytes 3076
  198.2 6.2 %copy-start.2 = (bf16[4,128,32,64]{1,0,3,2:T(4,128)(2,1)S(1)}, bf16[4,128,32,64]{1,0,3,2:T(4,128)(2,1)}, u32[]{:S(2)}) copy-start(bf16[4,128,32,64]{1,0,3,2:T(4,128)(2,1)} %multiply_convert_fusion.1) | copy-start | bytes 6291460
  243.8 24.2 %collective-permute-start.5 = (bf16[3,256]{1,0:T(4,128)(2,1)}, bf16[3,256]{1,0:T(4,128)(2,1)}, u32[]{:S(2)}, u32[]{:S(2)}) collective-permute-start(bf16[3,256]{1,0:T(4,128)(2,1)} %slice.183), channel_id=1, source_target_pairs={{8,0},{16,8},{24,16},{32,24},{40,32},{48,40},{56,48},{64,56},{72,6... | collective-permute-start | bytes 4616 | tf_op jit(solution)/shard_map/ppermute | solution.py:16
  261.1 6.8 %copy-start.32 = (f32[1,256]{1,0:T(1,128)S(1)}, f32[1,256]{1,0:T(1,128)}, u32[]{:S(2)}) copy-start(f32[1,256]{1,0:T(1,128)} %get-tuple-element.599) | copy-start | bytes 3076
  261.1 6.8 %copy-start.34 = (f32[1,256]{1,0:T(1,128)S(1)}, f32[1,256]{1,0:T(1,128)}, u32[]{:S(2)}) copy-start(f32[1,256]{1,0:T(1,128)} %get-tuple-element.600) | copy-start | bytes 3076
  261.1 6.8 %copy-start.36 = (f32[1,256]{1,0:T(1,128)S(1)}, f32[1,256]{1,0:T(1,128)}, u32[]{:S(2)}) copy-start(f32[1,256]{1,0:T(1,128)} %get-tuple-element.601) | copy-start | bytes 3076
  261.1 6.8 %copy-start.38 = (f32[1,256]{1,0:T(1,128)S(1)}, f32[1,256]{1,0:T(1,128)}, u32[]{:S(2)}) copy-start(f32[1,256]{1,0:T(1,128)} %get-tuple-element.602) | copy-start | bytes 3076
  418.0 6.2 %copy-start.3 = (f32[512,2048]{0,1:T(8,128)S(1)}, f32[512,2048]{0,1:T(8,128)}, u32[]{:S(2)}) copy-start(f32[512,2048]{0,1:T(8,128)} %get-tuple-element.587) | copy-start | bytes 12582916
  419.2 8.6 %collective-permute-start.4 = (bf16[3,256]{1,0:T(4,128)(2,1)S(1)}, bf16[3,256]{1,0:T(4,128)(2,1)S(1)}, u32[]{:S(2)}, u32[]{:S(2)}) collective-permute-start(bf16[3,256]{1,0:T(4,128)(2,1)S(1)} %slice.178), channel_id=1, source_target_pairs={{8,0},{16,8},{24,16},{32,24},{40,32},{48,40},{56,48},{64,56},{72,6... | collective-permute-start | bytes 4616 | tf_op jit(solution)/shard_map/ppermute | solution.py:16
  424.2 16.8 %copy-start.23 = (f32[1,2048]{1,0:T(1,128)S(1)}, f32[1,2048]{1,0:T(1,128)}, u32[]{:S(2)}) copy-start(f32[1,2048]{1,0:T(1,128)} %get-tuple-element.597) | copy-start | bytes 24580
  424.2 16.8 %copy-start.24 = (f32[1,2048]{1,0:T(1,128)S(1)}, f32[1,2048]{1,0:T(1,128)}, u32[]{:S(2)}) copy-start(f32[1,2048]{1,0:T(1,128)} %get-tuple-element.598) | copy-start | bytes 24580
  425.9 15.1 %collective-permute-start.3 = (bf16[3,2048]{0,1:T(8,128)(2,1)S(1)}, bf16[3,2048]{0,1:T(8,128)(2,1)S(1)}, u32[]{:S(2)}, u32[]{:S(2)}) collective-permute-start(bf16[3,2048]{0,1:T(8,128)(2,1)S(1)} %slice.173), channel_id=1, source_target_pairs={{8,0},{16,8},{24,16},{32,24},{40,32},{48,40},{56,48},{64,56},{72,6... | collective-permute-start | bytes 36872 | tf_op jit(solution)/shard_map/ppermute | solution.py:16
  (27 other events, 98.7 us)
Sparse Core Ops, SparseCore 0:
  65.0 113.2 all-gather.5
  222.6 133.4 all-gather.7
where the time goes:
time: 458 us; the launch traced here: 455 us
  waiting for transfers between devices  152 us (33%)
  other arithmetic  102 us (22%)
  local copies, waits for them, and re-layouts  95.3 us (21%)
  blocking collectives  36.9 us (8%)
  matrix products  34.4 us (8%)
  starting transfers between devices  18.7 us (4%)
  between operations  15.6 us (3%)
    all_gather x2, waiting for transfers between devices, entering(): lax.all_gather(a.astype(kind), axis)  139 us
    unnamed x1, blocking collectives  36.9 us
    dot_general x12, matrix products, product(): return jnp.einsum(form, left, right, preferred_element_type=jnp.float32)  34.4 us
    unnamed x110, local copies, waits for them, and re-layouts  26.5 us
    add x15, other arithmetic, combine_chain(): jnp.exp(later[0])[..., None, None] * earlier[1] + later[1]  24.5 us
    ppermute x6, starting transfers between devices, from_behind(): return lax.ppermute(array, axis, pairs)  18.6 us
    add x8, other arithmetic, advance(): return (jnp.exp(total_k)[..., None, None] * carried + state_k, carried)  16 us
    add x8, other arithmetic, retreat(): return (jnp.exp(total_k)[..., None, None] * carried + adj_k, carried)  16 us
  transfers between devices with their start and end apart: 8, of which 3 were waited for; matrix products, arithmetic and copies ran while one was open for 23% of the time, Pallas kernels for 0%

commit v1 on v0

v1 whole, which is shorter than its diff:
```python
import jax
import jax.numpy as jnp
from jax import lax
from jax.experimental import pallas as pl
from jax.experimental.pallas import tpu as pltpu
from jax.sharding import PartitionSpec as P

BLOCK = 128
NB = 4
T = 512
H = 32
W = 256
NQ = 8
ST = 256
HALO = 16
LROWS = ST + HALO
MESH = pl.DeviceIdType.MESH
F32 = jnp.float32
BF = jnp.bfloat16


def dot(a, b):
    return jnp.dot(a, b, preferred_element_type=F32)


def dot_nt(a, b):
    return lax.dot_general(a, b, (((1,), (1,)), ((), ())), preferred_element_type=F32)


def split3(v):
    hi = v.astype(BF)
    rest = v - hi.astype(F32)
    mid = rest.astype(BF)
    low = (rest - mid.astype(F32)).astype(BF)
    return hi, mid, low


def sigmoid(v):
    return 1.0 / (1.0 + jnp.exp(-v))


def tail_rows(row):
    hi, mid, low = split3(row)
    index = lax.broadcasted_iota(jnp.int32, (HALO, row.shape[1]), 0)
    zero = jnp.zeros((HALO, row.shape[1]), F32)
    full = jnp.where(
        index == 0,
        hi.astype(F32),
        jnp.where(index == 1, mid.astype(F32), jnp.where(index == 2, low.astype(F32), zero)),
    )
    return full.astype(BF)


def tail_sum(rows):
    return jnp.sum(rows.astype(F32), axis=0, keepdims=True)


def kernel(
    x_hbm, b_hbm, c_hbm, kx, kb, kc, step, dlog, skip, g_hbm,
    out_hbm, gx_hbm, gb_out, gc_out,
    xp, bp, cp, gs, cb, lh, cumt, ex, tot, ske,
    slope, growth, stte, acc_o, acc_g, sx, wx, gw, ls, la,
    gh, gpb, gpc, act_b, act_c, bt, ct, slope_b, slope_c,
    ps, sl, su, grad_b, grad_c,
    sf, sb, rf, rb, tf, tb, yf, yb, of, ob, inf, inb, rs_f, rs_b,
    in_sem, out_sem, halo_s, halo_r, ghalo_s, ghalo_r,
    f1s, f1r, b1s, b1r, yfs, yfr, ybs, ybr, f2s, f2r, b2s, b2r,
):
    me = lax.axis_index("context")
    y = me // 4
    x = me % 4
    nxt = (me + 1) % 16
    prv = (me + 15) % 16

    def remote(src, dst, s, r, peer):
        return pltpu.make_async_remote_copy(
            src_ref=src, dst_ref=dst, send_sem=s, recv_sem=r,
            device_id={"context": peer}, device_id_type=MESH,
        )

    barrier = pltpu.get_barrier_semaphore()
    peers = [nxt, prv]
    peers += [y * 4 + (x + r) % 4 for r in range(1, 4)]
    peers += [((y + r) % 4) * 4 + x for r in range(1, 4)]
    for peer in peers:
        pl.semaphore_signal(barrier, inc=1, device_id={"context": peer}, device_id_type=MESH)

    body = pl.ds(HALO, T)
    loads = [
        pltpu.make_async_copy(b_hbm, bp.at[body], in_sem.at[0]),
        pltpu.make_async_copy(c_hbm, cp.at[body], in_sem.at[1]),
        pltpu.make_async_copy(x_hbm, xp.at[body], in_sem.at[2]),
        pltpu.make_async_copy(g_hbm, gs, in_sem.at[3]),
    ]
    for load in loads:
        load.start()

    rate = -jnp.exp(dlog[...])
    lower = (
        lax.broadcasted_iota(jnp.int32, (BLOCK, BLOCK), 0)
        >= lax.broadcasted_iota(jnp.int32, (BLOCK, BLOCK), 1)
    )
    lower_f = lower.astype(F32)
    lower_b = lower_f.astype(BF)
    upper_f = (
        lax.broadcasted_iota(jnp.int32, (BLOCK, BLOCK), 0)
        <= lax.broadcasted_iota(jnp.int32, (BLOCK, BLOCK), 1)
    ).astype(F32)
    for b in range(NB):
        rows = pl.ds(b * BLOCK, BLOCK)
        step_b = step[rows, :]
        logs = split3(step_b * rate)
        cum = dot(lower_b, logs[0]) + dot(lower_b, logs[1]) + dot(lower_b, logs[2])
        pieces = split3(cum) + split3(step_b)
        lh[rows, :] = jnp.concatenate([p.astype(F32) for p in pieces], axis=1).astype(BF)
        flipped = jnp.transpose(cum)
        for q in range(NQ):
            cumt[q, 0:4, rows] = flipped[4 * q : 4 * q + 4]
    skips = split3(jnp.broadcast_to(skip[...], (16, H)))
    zero_s = jnp.zeros((16, 3 * H), F32)
    lh[pl.ds(T, 16), :] = jnp.concatenate(
        [p.astype(F32) for p in skips] + [zero_s], axis=1
    ).astype(BF)
    ps[...] = jnp.zeros_like(ps)
    grad_b[...] = jnp.zeros_like(grad_b)
    grad_c[...] = jnp.zeros_like(grad_c)

    pl.semaphore_wait(barrier, 8)

    head = pl.ds(0, HALO)
    last = pl.ds(T - HALO, HALO)
    halos = [
        remote(b_hbm.at[last], bp.at[head], halo_s.at[0], halo_r.at[0], nxt),
        remote(c_hbm.at[last], cp.at[head], halo_s.at[1], halo_r.at[1], nxt),
        remote(x_hbm.at[last], xp.at[head], halo_s.at[2], halo_r.at[2], nxt),
    ]

    @pl.when(me < 15)
    def _():
        for h in halos:
            h.start()

    @pl.when(me == 0)
    def _():
        for ref in (bp, cp, xp):
            ref[head, :] = jnp.zeros((HALO, ref.shape[1]), BF)

    for load in loads:
        load.wait()

    @pl.when(me > 0)
    def _():
        for h in halos:
            h.wait_recv()

    def conv(ref, lanes, taps):
        cb[...] = ref[:, lanes].astype(F32)
        pre = taps[0:1] * cb[pl.ds(13, T), :]
        for k in range(1, 4):
            pre = pre + taps[k : k + 1] * cb[pl.ds(13 + k, T), :]
        return pre

    all_bc = pl.ds(0, ST)
    for ref, taps, act, act_t, slo in (
        (bp, kb, act_b, bt, slope_b),
        (cp, kc, act_c, ct, slope_c),
    ):
        pre = conv(ref, all_bc, taps[...])
        sig = sigmoid(pre)
        slo[...] = sig * (1.0 + pre * (1.0 - sig))
        value = (pre * sig).astype(BF)
        act[...] = value
        for b in range(NB):
            act_t[b] = jnp.transpose(value[b * BLOCK : (b + 1) * BLOCK].astype(F32)).astype(BF)
    for b in range(NB):
        rows = pl.ds(b * BLOCK, BLOCK)
        scores = dot_nt(act_c[rows, :], act_b[rows, :])
        sl[b] = scores * lower_f
        su[b] = jnp.transpose(scores) * upper_f

    def blk(b):
        return pl.ds(b * BLOCK, BLOCK)

    def lanes_of(q):
        return pl.ds(pl.multiple_of(q * W, W), W)

    def order(p):
        r = (p % 4 + 1) % 4
        k = p // 4
        return r, k, ((x + r) % 4) * 2 + k

    def row_peer(r):
        return y * 4 + (x + r) % 4

    def f1(r, k):
        return remote(
            sf.at[((x + r) % 4) * 2 + k], rf.at[x * 2 + k], f1s.at[r, k], f1r.at[r, k], row_peer(r)
        )

    def b1(r, k):
        return remote(
            sb.at[((x + r) % 4) * 2 + k], rb.at[x * 2 + k], b1s.at[r, k], b1r.at[r, k], row_peer(r)
        )

    def f2(r, k):
        return remote(
            of.at[((x + r) % 4) * 2 + k], inf.at[x * 2 + k], f2s.at[r, k], f2r.at[r, k], row_peer(r)
        )

    def b2(r, k):
        return remote(
            ob.at[((x + r) % 4) * 2 + k], inb.at[x * 2 + k], b2s.at[r, k], b2r.at[r, k], row_peer(r)
        )

    def yf_cp(r, k):
        return remote(
            tf.at[k], yf.at[y * 2 + k], yfs.at[r, k], yfr.at[y, k], ((y + r) % 4) * 4 + x
        )

    def yb_cp(r, k):
        return remote(
            tb.at[k], yb.at[y * 2 + k], ybs.at[r, k], ybr.at[y, k], ((y + r) % 4) * 4 + x
        )

    def forward_local(p, carry):
        r, k, q = order(p)
        lanes = lanes_of(q)
        depth = lax.broadcasted_iota(jnp.int32, (6 * H, 2 * W), 0)
        col = lax.broadcasted_iota(jnp.int32, (6 * H, 2 * W), 1)
        hit = (depth % H == 4 * q + (col % W) // 64) & ((depth // (3 * H)) == (col // W))
        ex[...] = dot(lh[...], hit.astype(F32).astype(BF))
        ske[q] = ex[pl.ds(T, 8), 0:W]
        pre = conv(xp, lanes, kx[:, lanes])
        sig = sigmoid(pre)
        slope[q] = sig * (1.0 + pre * (1.0 - sig))
        act = (pre * sig).astype(BF).astype(F32)
        cum = ex[pl.ds(0, T), 0:W]
        steps = ex[pl.ds(0, T), W : 2 * W]
        acc_o[q] = act * ex[pl.ds(T, 1), 0:W]
        acc_g[q] = steps
        growth[q] = jnp.exp(cum)
        scaled = (act * steps).astype(BF)
        sx[q] = scaled
        state = None
        total = None
        for b in range(NB):
            tot_b = ex[pl.ds(b * BLOCK + BLOCK - 1, 1), 0:W]
            tot[q, pl.ds(b, 1), :] = tot_b
            to_end = jnp.exp(tot_b - ex[blk(b), 0:W])
            stte[q, blk(b), :] = ex[blk(b), W : 2 * W] * to_end
            weighted = (scaled[b * BLOCK : (b + 1) * BLOCK].astype(F32) * to_end).astype(BF)
            wx[q, blk(b), :] = weighted
            grown = dot(bt[b], weighted)
            if b == 0:
                state, total = grown, tot_b
            else:
                ls[q, b - 1] = state
                state = jnp.exp(tot_b) * state + grown
                total = total + tot_b
        state = state.astype(BF)
        tail = tail_rows(total)

        @pl.when(r == 0)
        def _():
            rf[q, 0:ST, :] = state
            rf[q, ST:LROWS, :] = tail

        @pl.when(r > 0)
        def _():
            sf[q, 0:ST, :] = state
            sf[q, ST:LROWS, :] = tail
            f1(r, k).start()

        return carry

    lax.fori_loop(0, NQ, forward_local, 0)

    def backward_local(p, carry):
        r, k, q = order(p)
        lanes = lanes_of(q)
        state = None
        for b in reversed(range(NB)):
            grads = (gs[blk(b), lanes].astype(F32) * growth[q, blk(b), :]).astype(BF)
            gw[q, blk(b), :] = grads
            grown = dot(ct[b], grads)
            if b == NB - 1:
                state = jnp.exp(tot[q, pl.ds(b, 1), :]) * 0.0 + grown
            else:
                la[q, b] = state
                state = jnp.exp(tot[q, pl.ds(b, 1), :]) * state + grown
        state = state.astype(BF)

        @pl.when(r == 0)
        def _():
            rb[q] = state

        @pl.when(r > 0)
        def _():
            sb[q] = state
            b1(r, k).start()

        return carry

    lax.fori_loop(0, NQ, backward_local, 0)

    left = lax.broadcasted_iota(jnp.int32, (BLOCK, BLOCK), 1) < 64

    def halves(value):
        zero = jnp.zeros_like(value)
        return jnp.concatenate([jnp.where(left, value, zero), jnp.where(left, zero, value)], axis=0)

    def intra(q, carry):
        depth = lax.broadcasted_iota(jnp.int32, (6 * H, 2 * W), 0)
        col = lax.broadcasted_iota(jnp.int32, (6 * H, 2 * W), 1)
        hit = (depth % H == 4 * q + col // BLOCK) & (depth < 3 * H)
        hit = hit.astype(F32).astype(BF)
        for b in range(NB):
            down = dot(lh[blk(b), :], hit)
            for pair in range(2):
                part = pl.ds(pair * BLOCK, BLOCK)
                across = jnp.concatenate(
                    [cumt[q, pl.ds(2 * pair + i, 1), blk(b)] for i in range(2)], axis=1
                )
                differ = down[:, pair * W : (pair + 1) * W] - across
                table = jnp.exp(-jnp.abs(differ))
                scores = jnp.concatenate([sl[b], sl[b]], axis=1)
                scores_t = jnp.concatenate([su[b], su[b]], axis=1)
                mixing = (table * scores).astype(BF)
                mixing_t = (table * scores_t).astype(BF)
                scaled = sx[q, blk(b), part]
                grads = gs[blk(b), pl.ds(pl.multiple_of(q * W + pair * BLOCK, BLOCK), BLOCK)]
                wide_x = halves(scaled)
                acc_o[q, blk(b), part] += dot(mixing, wide_x)
                inner = dot(mixing_t, halves(grads))
                acc_g[q, blk(b), part] = (
                    acc_g[q, blk(b), part] * inner + ske[q, 0:1, part] * grads.astype(F32)
                )
                both = table * dot_nt(grads, wide_x)
                ps[b] += both[:, :BLOCK] + both[:, BLOCK:]
        return carry

    def row_forward(k):
        state, total = None, None
        for i in range(4):
            local = rf[i * 2 + k, 0:ST, :].astype(F32)
            own = tail_sum(rf[i * 2 + k, ST:LROWS, :])
            if i == 0:
                state, total = local, own
            else:
                state = jnp.exp(own) * state + local
                total = total + own
        tf[k, 0:ST, :] = state.astype(BF)
        tf[k, ST:LROWS, :] = tail_rows(total)
        rs_f[k] = jnp.zeros((ST, W), F32)
        for r in range(1, 4):
            @pl.when(y + r <= 3)
            def _():
                yf_cp(r, k).start()

    def row_backward(k):
        state = None
        for i in reversed(range(4)):
            local = rb[i * 2 + k].astype(F32)
            own = tail_sum(rf[i * 2 + k, ST:LROWS, :])
            state = local if i == 3 else jnp.exp(own) * state + local
        tb[k, 0:ST, :] = state.astype(BF)
        tb[k, ST:LROWS, :] = tf[k, ST:LROWS, :]
        rs_b[k] = jnp.zeros((ST, W), F32)
        for r in range(1, 4):
            @pl.when(y - (4 - r) >= 0)
            def _():
                yb_cp(r, k).start()

    def finish_forward(k):
        for i in range(3):
            @pl.when(i < y)
            def _():
                remote(
                    tf.at[k], yf.at[i * 2 + k], yfs.at[1, k], yfr.at[i, k], nxt
                ).wait_recv()
                own = tail_sum(yf[i * 2 + k, ST:LROWS, :])
                rs_f[k] = jnp.exp(own) * rs_f[k] + yf[i * 2 + k, 0:ST, :].astype(F32)
        state = rs_f[k]
        for i in range(4):
            out = state.astype(BF)
            of[i * 2 + k] = out

            @pl.when(x == i)
            def _():
                inf[i * 2 + k] = out

            if i < 3:
                own = tail_sum(rf[i * 2 + k, ST:LROWS, :])
                state = jnp.exp(own) * state + rf[i * 2 + k, 0:ST, :].astype(F32)
        for r in range(1, 4):
            f2(r, k).start()

    def finish_backward(k):
        for i in reversed(range(1, 4)):
            @pl.when(i > y)
            def _():
                remote(
                    tb.at[k], yb.at[i * 2 + k], ybs.at[1, k], ybr.at[i, k], nxt
                ).wait_recv()
                own = tail_sum(yb[i * 2 + k, ST:LROWS, :])
                rs_b[k] = jnp.exp(own) * rs_b[k] + yb[i * 2 + k, 0:ST, :].astype(F32)
        state = rs_b[k]
        for i in reversed(range(4)):
            out = state.astype(BF)
            ob[i * 2 + k] = out

            @pl.when(x == i)
            def _():
                inb[i * 2 + k] = out

            if i > 0:
                own = tail_sum(rf[i * 2 + k, ST:LROWS, :])
                state = jnp.exp(own) * state + rb[i * 2 + k].astype(F32)
        for r in range(1, 4):
            b2(r, k).start()

    lax.fori_loop(0, 3, intra, 0)
    for k in range(2):
        for r in range(1, 4):
            f1(r, k).wait_recv()
        row_forward(k)
    lax.fori_loop(3, 7, intra, 0)
    for k in range(2):
        finish_forward(k)
    for k in range(2):
        for r in range(1, 4):
            b1(r, k).wait_recv()
        row_backward(k)
    lax.fori_loop(7, 8, intra, 0)
    for k in range(2):
        finish_backward(k)

    def order_in(p):
        r = p % 4
        k = p // 4
        return r, k, ((x + 4 - r) % 4) * 2 + k

    def out_copy(q):
        return pltpu.make_async_copy(sx.at[q], out_hbm.at[:, lanes_of(q)], out_sem.at[0, q])

    def gx_copy(q):
        return pltpu.make_async_copy(wx.at[q], gx_hbm.at[:, lanes_of(q)], out_sem.at[1, q])

    def enter_forward(p, carry):
        r, k, q = order_in(p)

        @pl.when(r > 0)
        def _():
            f2(r, k).wait_recv()

        start = inf[q]
        base = start.astype(F32)
        total = None
        for b in range(NB):
            if b > 0:
                tot_b = tot[q, pl.ds(b - 1, 1), :]
                total = tot_b if b == 1 else total + tot_b
                start = (ls[q, b - 1] + jnp.exp(total) * base).astype(BF)
            carried = growth[q, blk(b), :] * dot(act_c[blk(b), :], start)
            sx[q, blk(b), :] = (acc_o[q, blk(b), :] + carried).astype(BF)
            grad_c[blk(b), :] += dot_nt(gw[q, blk(b), :], start)
        out_copy(q).start()
        return carry

    lax.fori_loop(0, NQ, enter_forward, 0)

    def back_conv(value, halo, taps):
        cb[pl.ds(0, T), :] = value
        cb[pl.ds(T, HALO), :] = halo
        grad = taps[0:1] * cb[pl.ds(3, T), :]
        for k in range(1, 4):
            grad = grad + taps[k : k + 1] * cb[pl.ds(3 - k, T), :]
        return grad.astype(BF)

    tail = pl.ds(T, HALO)

    def ghalo(src, dst, slot):
        return remote(src, dst, ghalo_s.at[slot], ghalo_r.at[slot], prv)

    def ghalo_x(q):
        return ghalo(gs.at[head, lanes_of(q)], gh.at[q], q)

    def ghalo_b():
        return ghalo(gpb.at[head], gpb.at[tail], NQ)

    def ghalo_c():
        return ghalo(gpc.at[head], gpc.at[tail], NQ + 1)

    def send_halo(copy):
        @pl.when(me > 0)
        def _():
            copy.start()

    def take_halo(copy, dst):
        @pl.when(me < 15)
        def _():
            copy.wait_recv()

        @pl.when(me == 15)
        def _():
            dst[...] = jnp.zeros((HALO, W), BF)

    def finish_x(p):
        q = order_in(p)[2]
        take_halo(ghalo_x(q), gh.at[q])
        wx[q] = back_conv(gs[:, lanes_of(q)].astype(F32), gh[q].astype(F32), kx[:, lanes_of(q)])
        gx_copy(q).start()

    def enter_backward(p, carry):
        r, k, q = order_in(p)

        @pl.when(r > 0)
        def _():
            b2(r, k).wait_recv()

        after = inb[q]
        base = after.astype(F32)
        total = None
        for b in reversed(range(NB)):
            if b < NB - 1:
                tot_b = tot[q, pl.ds(b + 1, 1), :]
                total = tot_b if b == NB - 2 else total + tot_b
                after = (la[q, b] + jnp.exp(total) * base).astype(BF)
            outer = stte[q, blk(b), :] * dot(act_b[blk(b), :], after)
            grads = (acc_g[q, blk(b), :] + outer) * slope[q, blk(b), :]
            gs[blk(b), lanes_of(q)] = grads.astype(BF)
            grad_b[blk(b), :] += dot_nt(wx[q, blk(b), :], after)
        send_halo(ghalo_x(q))

        @pl.when(p > 0)
        def _():
            finish_x(p - 1)

        return carry

    lax.fori_loop(0, NQ, enter_backward, 0)

    for b in range(NB):
        pair_sum = ps[b] * lower_f
        pair_t = jnp.transpose(pair_sum).astype(BF)
        pair_sum = pair_sum.astype(BF)
        into_b = grad_b[blk(b), :] + dot(pair_t, act_c[blk(b), :])
        into_c = grad_c[blk(b), :] + dot(pair_sum, act_b[blk(b), :])
        gpb[blk(b), :] = (into_b * slope_b[blk(b), :]).astype(BF)
        gpc[blk(b), :] = (into_c * slope_c[blk(b), :]).astype(BF)
    send_halo(ghalo_b())
    send_halo(ghalo_c())
    finish_x(NQ - 1)
    for ref, taps, out, copy in ((gpb, kb, gb_out, ghalo_b()), (gpc, kc, gc_out, ghalo_c())):
        take_halo(copy, ref.at[tail])
        out[...] = back_conv(
            ref[pl.ds(0, T), :].astype(F32), ref[tail, :].astype(F32), taps[...]
        )

    for q in range(NQ):
        out_copy(q).wait()
        gx_copy(q).wait()

    @pl.when(me < 15)
    def _():
        for h in halos:
            h.wait_send()

    @pl.when(me > 0)
    def _():
        for q in range(NQ):
            ghalo_x(q).wait_send()
        ghalo_b().wait_send()
        ghalo_c().wait_send()

    for k in range(2):
        for r in range(1, 4):
            f1(r, k).wait_send()
            b1(r, k).wait_send()
            f2(r, k).wait_send()
            b2(r, k).wait_send()

            @pl.when(y + r <= 3)
            def _():
                yf_cp(r, k).wait_send()

            @pl.when(y - (4 - r) >= 0)
            def _():
                yb_cp(r, k).wait_send()


def on_device(x, b, c, kx, kb, kc, step, dlog, skip, g):
    hbm = pl.BlockSpec(memory_space=pl.ANY)
    vmem = pl.BlockSpec(memory_space=pltpu.VMEM)
    dma = pltpu.SemaphoreType.DMA
    full = (NQ, T, W)
    scratch = [
        pltpu.VMEM((T + HALO, NQ * W), BF),
        pltpu.VMEM((T + HALO, ST), BF),
        pltpu.VMEM((T + HALO, ST), BF),
        pltpu.VMEM((T, NQ * W), BF),
        pltpu.VMEM((T + HALO, W), F32),
        pltpu.VMEM((T + 16, 6 * H), BF),
        pltpu.VMEM((NQ, 8, T), F32),
        pltpu.VMEM((T + 16, 2 * W), F32),
        pltpu.VMEM((NQ, 8, W), F32),
        pltpu.VMEM((NQ, 8, W), F32),
        pltpu.VMEM(full, F32),
        pltpu.VMEM(full, F32),
        pltpu.VMEM(full, F32),
        pltpu.VMEM(full, F32),
        pltpu.VMEM(full, F32),
        pltpu.VMEM(full, BF),
        pltpu.VMEM(full, BF),
        pltpu.VMEM(full, BF),
        pltpu.VMEM((NQ, 3, ST, W), F32),
        pltpu.VMEM((NQ, 3, ST, W), F32),
        pltpu.VMEM((NQ, HALO, W), BF),
        pltpu.VMEM((T + HALO, ST), BF),
        pltpu.VMEM((T + HALO, ST), BF),
        pltpu.VMEM((T, ST), BF),
        pltpu.VMEM((T, ST), BF),
        pltpu.VMEM((NB, ST, BLOCK), BF),
        pltpu.VMEM((NB, ST, BLOCK), BF),
        pltpu.VMEM((T, ST), F32),
        pltpu.VMEM((T, ST), F32),
        pltpu.VMEM((NB, BLOCK, BLOCK), F32),
        pltpu.VMEM((NB, BLOCK, BLOCK), F32),
        pltpu.VMEM((NB, BLOCK, BLOCK), F32),
        pltpu.VMEM((T, ST), F32),
        pltpu.VMEM((T, ST), F32),
        pltpu.VMEM((NQ, LROWS, W), BF),
        pltpu.VMEM((NQ, ST, W), BF),
        pltpu.VMEM((NQ, LROWS, W), BF),
        pltpu.VMEM((NQ, ST, W), BF),
        pltpu.VMEM((2, LROWS, W), BF),
        pltpu.VMEM((2, LROWS, W), BF),
        pltpu.VMEM((NQ, LROWS, W), BF),
        pltpu.VMEM((NQ, LROWS, W), BF),
        pltpu.VMEM((NQ, ST, W), BF),
        pltpu.VMEM((NQ, ST, W), BF),
        pltpu.VMEM((NQ, ST, W), BF),
        pltpu.VMEM((NQ, ST, W), BF),
        pltpu.VMEM((2, ST, W), F32),
        pltpu.VMEM((2, ST, W), F32),
        dma((4,)), dma((2, NQ)), dma((3,)), dma((3,)), dma((10,)), dma((10,)),
    ] + [dma((4, 2))] * 12
    return pl.pallas_call(
        kernel,
        out_shape=(
            jax.ShapeDtypeStruct(x.shape, BF),
            jax.ShapeDtypeStruct(x.shape, BF),
            jax.ShapeDtypeStruct(b.shape, BF),
            jax.ShapeDtypeStruct(c.shape, BF),
        ),
        in_specs=[hbm] * 3 + [vmem] * 6 + [hbm],
        out_specs=(hbm, hbm, vmem, vmem),
        scratch_shapes=scratch,
        compiler_params=pltpu.CompilerParams(
            collective_id=0, has_side_effects=True, vmem_limit_bytes=67043328
        ),
    )(x, b, c, kx, kb, kc, step, dlog.reshape(1, H), skip.reshape(1, H), g)


def solution(mesh):
    rows = P(("doc", "context"), "head")
    taps = P(None, "head")
    return jax.shard_map(
        on_device,
        mesh=mesh,
        in_specs=(rows, rows, rows, taps, taps, taps, rows, P("head"), P("head"), rows),
        out_specs=(rows, rows, rows, rows),
        check_vma=False,
    )
```

time: 458 us -> 99.3 us (0.22)
  waiting for transfers between devices: 152 us -> 0 us
  other arithmetic: 102 us -> 0 us
  Pallas kernels: 0 us -> 89.7 us
  local copies, waits for them, and re-layouts: 95.3 us -> 7.72 us
  blocking collectives: 36.9 us -> 0 us
  matrix products: 34.4 us -> 0 us
  starting transfers between devices: 18.7 us -> 0 us
  between operations: 15.6 us -> 0.65 us
    all_gather x2 -> x0, waiting for transfers between devices: 139 us -> none  [entering(): lax.all_gather(a.astype(kind), axis)]
    pallas_call x0 -> x1, Pallas kernels: none -> 89.7 us  [on_device(): pl.pallas_call(kernel, out_shape=(jax.ShapeDtypeStruct(x.shape, BF), jax....]
    add x31 -> x0, other arithmetic: 56.5 us -> none  [the longest x15 24.5 us: combine_chain(): jnp.exp(later[0])[..., None, None] * earlier[1] + later[1]]
    unnamed x1 -> x0, blocking collectives: 36.9 us -> none
    dot_general x12 -> x0, matrix products: 34.4 us -> none  [product(): return jnp.einsum(form, left, right, preferred_element_type=jnp.float32)]
    convert_element_type x13 -> x0, other arithmetic: 32.8 us -> none  [the longest x2 14 us: prepare(): scaled_x = (blk_x * step_block[..., None]).astype(jnp.bfloat16)]
    convert_element_type x4 -> x0, local copies, waits for them, and re-layouts: 25.9 us -> none  [the longest x2 15.4 us: prepare(): grad_weighted = (grad_block * growth[..., None]).astype(jnp.bfloat16)]
    unnamed x110 -> x11, local copies, waits for them, and re-layouts: 26.5 us -> 7.72 us
  transfers between devices with their start and end apart: 8 -> 0, of which waited for: 3 -> 0; matrix products, arithmetic and copies ran while one was open for 23% -> 0% of each run, Pallas kernels for 0% -> 0%
where the time goes in v1:
time: 99.3 us; the launch traced here: 98.1 us
  Pallas kernels  89.7 us (90%)
  local copies, waits for them, and re-layouts  7.72 us (8%)
    pallas_call x1, Pallas kernels, on_device(): pl.pallas_call(kernel, out_shape=(jax.ShapeDtypeStruct(x.shape, BF), jax....  89.7 us
    unnamed x11, local copies, waits for them, and re-layouts  7.72 us

profile of v1, /device:TPU:2, one launch (start us, length us, event | category | flops | bytes accessed | tf_op | source)
XLA Modules:
  0.0 98.1 jit_solution(3755424407191555533)
XLA Ops:
  0.6 1.7 %copy.14.step = f32[512,32]{1,0:T(8,128)} copy(f32[512,32]{0,1:T(8,128)} %param.16) | data formatting | bytes 131072 | tf_op args[6]
  2.3 89.7 %shard_map.129 = (bf16[512,2048]{1,0:T(8,128)(2,1)}, bf16[512,2048]{1,0:T(8,128)(2,1)}, bf16[512,256]{1,0:T(8,128)(2,1)}, bf16[512,256]{1,0:T(8,128)(2,1)}) custom-call(bf16[512,2048]{1,0:T(8,128)(2,1)} %x_hbm.1, bf16[512,256]{1,0:T(8,128)(2,1)} %b_hbm.1, bf16[512,256]{1,0:T(8,128)(2,1)} %c_hbm.1, f32[4,2048]{1,0:T(4,128)} %kx.1, f32[4,256]{1,0:T(4,128)} %kb.1, ...), custom_call_target="tpu_custom_call" | custom-call | tf_op jit(solution)/shard_map/pallas_call | solution.py:648
  92.0 0.0 copy-start
  92.0 3.3 %copy.19 = bf16[512,2048]{1,0:T(8,128)(2,1)} copy(bf16[512,2048]{1,0:T(8,128)(2,1)} %get-tuple-element.8) | data formatting | bytes 4194304
  95.4 0.0 copy-done
  95.4 0.0 copy-start.2
  95.4 0.0 copy-start.1
  95.4 1.3 %copy.20 = bf16[512,2048]{1,0:T(8,128)(2,1)} copy(bf16[512,2048]{1,0:T(8,128)(2,1)S(1)} %copy-done) | data formatting | bytes 4194304
  96.7 0.0 copy-done.2
  96.7 0.7 copy.21
  97.4 0.0 copy-done.1
  97.4 0.7 copy.22
Async XLA Ops:
  92.0 3.3 %copy-start = (bf16[512,2048]{1,0:T(8,128)(2,1)S(1)}, bf16[512,2048]{1,0:T(8,128)(2,1)}, u32[]{:S(2)}) copy-start(bf16[512,2048]{1,0:T(8,128)(2,1)} %get-tuple-element.9) | copy-start | bytes 6291460
  95.4 1.3 %copy-start.2 = (bf16[512,256]{1,0:T(8,128)(2,1)S(1)}, bf16[512,256]{1,0:T(8,128)(2,1)}, u32[]{:S(2)}) copy-start(bf16[512,256]{1,0:T(8,128)(2,1)} %get-tuple-element.10) | copy-start | bytes 786436
  95.4 2.0 %copy-start.1 = (bf16[512,256]{1,0:T(8,128)(2,1)S(1)}, bf16[512,256]{1,0:T(8,128)(2,1)}, u32[]{:S(2)}) copy-start(bf16[512,256]{1,0:T(8,128)(2,1)} %get-tuple-element.11) | copy-start | bytes 786436

commit v2 on v1

--- a/solution.py
+++ b/solution.py
@@ -57,7 +57,7 @@
 
 def kernel(
     x_hbm, b_hbm, c_hbm, kx, kb, kc, step, dlog, skip, g_hbm,
-    out_hbm, gx_hbm, gb_out, gc_out,
+    out_hbm, gp_hbm, gh_out, gpb_out, gpc_out,
     xp, bp, cp, gs, cb, lh, cumt, ex, tot, ske,
     slope, growth, stte, acc_o, acc_g, sx, wx, gw, ls, la,
     gh, gpb, gpc, act_b, act_c, bt, ct, slope_b, slope_c,
@@ -95,27 +95,26 @@
     for load in loads:
         load.start()
 
-    rate = -jnp.exp(dlog[...])
+    rate = -jnp.exp(jnp.transpose(jnp.broadcast_to(dlog[...], (8, H)))[:, 0:1])
     lower = (
         lax.broadcasted_iota(jnp.int32, (BLOCK, BLOCK), 0)
         >= lax.broadcasted_iota(jnp.int32, (BLOCK, BLOCK), 1)
     )
     lower_f = lower.astype(F32)
-    lower_b = lower_f.astype(BF)
     upper_f = (
         lax.broadcasted_iota(jnp.int32, (BLOCK, BLOCK), 0)
         <= lax.broadcasted_iota(jnp.int32, (BLOCK, BLOCK), 1)
     ).astype(F32)
+    upper_b = upper_f.astype(BF)
     for b in range(NB):
         rows = pl.ds(b * BLOCK, BLOCK)
-        step_b = step[rows, :]
+        step_b = step[:, rows]
         logs = split3(step_b * rate)
-        cum = dot(lower_b, logs[0]) + dot(lower_b, logs[1]) + dot(lower_b, logs[2])
-        pieces = split3(cum) + split3(step_b)
-        lh[rows, :] = jnp.concatenate([p.astype(F32) for p in pieces], axis=1).astype(BF)
-        flipped = jnp.transpose(cum)
+        flipped = dot(logs[0], upper_b) + dot(logs[1], upper_b) + dot(logs[2], upper_b)
         for q in range(NQ):
             cumt[q, 0:4, rows] = flipped[4 * q : 4 * q + 4]
+        pieces = split3(jnp.transpose(flipped)) + split3(jnp.transpose(step_b))
+        lh[rows, :] = jnp.concatenate([p.astype(F32) for p in pieces], axis=1).astype(BF)
     skips = split3(jnp.broadcast_to(skip[...], (16, H)))
     zero_s = jnp.zeros((16, 3 * H), F32)
     lh[pl.ds(T, 16), :] = jnp.concatenate(
@@ -443,8 +442,9 @@
     def out_copy(q):
         return pltpu.make_async_copy(sx.at[q], out_hbm.at[:, lanes_of(q)], out_sem.at[0, q])
 
-    def gx_copy(q):
-        return pltpu.make_async_copy(wx.at[q], gx_hbm.at[:, lanes_of(q)], out_sem.at[1, q])
+    def gp_copy(q):
+        lanes = lanes_of(q)
+        return pltpu.make_async_copy(gs.at[:, lanes], gp_hbm.at[:, lanes], out_sem.at[1, q])
 
     def enter_forward(p, carry):
         r, k, q = order_in(p)
@@ -469,14 +469,6 @@
 
     lax.fori_loop(0, NQ, enter_forward, 0)
 
-    def back_conv(value, halo, taps):
-        cb[pl.ds(0, T), :] = value
-        cb[pl.ds(T, HALO), :] = halo
-        grad = taps[0:1] * cb[pl.ds(3, T), :]
-        for k in range(1, 4):
-            grad = grad + taps[k : k + 1] * cb[pl.ds(3 - k, T), :]
-        return grad.astype(BF)
-
     tail = pl.ds(T, HALO)
 
     def ghalo(src, dst, slot):
@@ -504,12 +496,6 @@
         @pl.when(me == 15)
         def _():
             dst[...] = jnp.zeros((HALO, W), BF)
-
-    def finish_x(p):
-        q = order_in(p)[2]
-        take_halo(ghalo_x(q), gh.at[q])
-        wx[q] = back_conv(gs[:, lanes_of(q)].astype(F32), gh[q].astype(F32), kx[:, lanes_of(q)])
-        gx_copy(q).start()
 
     def enter_backward(p, carry):
         r, k, q = order_in(p)
@@ -531,11 +517,7 @@
             gs[blk(b), lanes_of(q)] = grads.astype(BF)
             grad_b[blk(b), :] += dot_nt(wx[q, blk(b), :], after)
         send_halo(ghalo_x(q))
-
-        @pl.when(p > 0)
-        def _():
-            finish_x(p - 1)
-
+        gp_copy(q).start()
         return carry
 
     lax.fori_loop(0, NQ, enter_backward, 0)
@@ -550,16 +532,18 @@
         gpc[blk(b), :] = (into_c * slope_c[blk(b), :]).astype(BF)
     send_halo(ghalo_b())
     send_halo(ghalo_c())
-    finish_x(NQ - 1)
-    for ref, taps, out, copy in ((gpb, kb, gb_out, ghalo_b()), (gpc, kc, gc_out, ghalo_c())):
+    gpb_out[pl.ds(0, T), :] = gpb[pl.ds(0, T), :]
+    gpc_out[pl.ds(0, T), :] = gpc[pl.ds(0, T), :]
+    for q in range(NQ):
+        take_halo(ghalo_x(q), gh.at[q])
+        gh_out[:, q * W : (q + 1) * W] = gh[q]
+    for ref, out, copy in ((gpb, gpb_out, ghalo_b()), (gpc, gpc_out, ghalo_c())):
         take_halo(copy, ref.at[tail])
-        out[...] = back_conv(
-            ref[pl.ds(0, T), :].astype(F32), ref[tail, :].astype(F32), taps[...]
-        )
+        out[tail, :] = ref[tail, :]
 
     for q in range(NQ):
         out_copy(q).wait()
-        gx_copy(q).wait()
+        gp_copy(q).wait()
 
     @pl.when(me < 15)
     def _():
@@ -587,6 +571,25 @@
             @pl.when(y - (4 - r) >= 0)
             def _():
                 yb_cp(r, k).wait_send()
+
+
+def back_kernel(out, gp, gh, gpb, gpc, kx, kb, kc, out_ref, gx_ref, gb_ref, gc_ref, cb):
+    def back(taps):
+        grad = taps[0:1] * cb[pl.ds(3, T), :]
+        for k in range(1, 4):
+            grad = grad + taps[k : k + 1] * cb[pl.ds(3 - k, T), :]
+        return grad.astype(BF)
+
+    out_ref[...] = out[...]
+    cb[pl.ds(0, T), :] = gp[...].astype(F32)
+    cb[pl.ds(T, HALO), :] = gh[...].astype(F32)
+    gx_ref[...] = back(kx[...])
+
+    @pl.when(pl.program_id(0) == 0)
+    def _():
+        for ref, taps, res in ((gpb, kb, gb_ref), (gpc, kc, gc_ref)):
+            cb[...] = ref[...].astype(F32)
+            res[...] = back(taps[...])
 
 
 def on_device(x, b, c, kx, kb, kc, step, dlog, skip, g):
@@ -645,21 +648,42 @@
         pltpu.VMEM((2, ST, W), F32),
         dma((4,)), dma((2, NQ)), dma((3,)), dma((3,)), dma((10,)), dma((10,)),
     ] + [dma((4, 2))] * 12
+    out, gp, gh, gpb, gpc = pl.pallas_call(
+        kernel,
+        out_shape=(
+            jax.ShapeDtypeStruct(x.shape, BF),
+            jax.ShapeDtypeStruct(x.shape, BF),
+            jax.ShapeDtypeStruct((HALO, NQ * W), BF),
+            jax.ShapeDtypeStruct((T + HALO, ST), BF),
+            jax.ShapeDtypeStruct((T + HALO, ST), BF),
+        ),
+        in_specs=[hbm] * 3 + [vmem] * 6 + [hbm],
+        out_specs=(hbm, hbm, vmem, vmem, vmem),
+        scratch_shapes=scratch,
+        compiler_params=pltpu.CompilerParams(
+            collective_id=0, has_side_effects=True, vmem_limit_bytes=67043328
+        ),
+    )(x, b, c, kx, kb, kc, step.T, dlog.reshape(1, H), skip.reshape(1, H), g)
+    slab = pl.BlockSpec((T, W), lambda q: (0, q))
+    whole = pl.BlockSpec((T, ST), lambda q: (0, 0))
+    padded = pl.BlockSpec((T + HALO, ST), lambda q: (0, 0))
+    small = pl.BlockSpec((4, ST), lambda q: (0, 0))
     return pl.pallas_call(
-        kernel,
+        back_kernel,
+        grid=(NQ,),
         out_shape=(
             jax.ShapeDtypeStruct(x.shape, BF),
             jax.ShapeDtypeStruct(x.shape, BF),
             jax.ShapeDtypeStruct(b.shape, BF),
             jax.ShapeDtypeStruct(c.shape, BF),
         ),
-        in_specs=[hbm] * 3 + [vmem] * 6 + [hbm],
-        out_specs=(hbm, hbm, vmem, vmem),
-        scratch_shapes=scratch,
-        compiler_params=pltpu.CompilerParams(
-            collective_id=0, has_side_effects=True, vmem_limit_bytes=67043328
-        ),
-    )(x, b, c, kx, kb, kc, step, dlog.reshape(1, H), skip.reshape(1, H), g)
+        in_specs=[
+            slab, slab, pl.BlockSpec((HALO, W), lambda q: (0, q)), padded, padded,
+            pl.BlockSpec((4, W), lambda q: (0, q)), small, small,
+        ],
+        out_specs=(slab, slab, whole, whole),
+        scratch_shapes=[pltpu.VMEM((T + HALO, W), F32)],
+    )(out, gp, gh, gpb, gpc, kx, kb, kc)
 
 
 def solution(mesh):

time: 99.3 us -> 81.8 us (0.82)
  Pallas kernels: 89.7 us -> 80.8 us
  local copies, waits for them, and re-layouts: 7.72 us -> 0 us
    pallas_call x1, Pallas kernels: 89.7 us -> 71.1 us  [on_device(): pl.pallas_call(kernel, out_shape=(jax.ShapeDtypeStruct(x.shape, BF), jax....]
    pallas_call x0 -> x1, Pallas kernels: none -> 9.74 us  [on_device(): pl.pallas_call(back_kernel, grid=(NQ,), out_shape=(jax.ShapeDtypeStruct(x...]
    unnamed x11 -> x0, local copies, waits for them, and re-layouts: 7.72 us -> none
where the time goes in v2:
time: 81.8 us; the launch traced here: 81.5 us
  Pallas kernels  80.8 us (99%)
    pallas_call x1, Pallas kernels, on_device(): pl.pallas_call(kernel, out_shape=(jax.ShapeDtypeStruct(x.shape, BF), jax....  71.1 us
    pallas_call x1, Pallas kernels, on_device(): pl.pallas_call(back_kernel, grid=(NQ,), out_shape=(jax.ShapeDtypeStruct(x...  9.74 us

profile of v2, /device:TPU:2, one launch (start us, length us, event | category | flops | bytes accessed | tf_op | source)
XLA Modules:
  0.0 81.5 jit_solution(14333719371948668450)
XLA Ops:
  0.6 71.1 %shard_map.129 = (bf16[512,2048]{1,0:T(8,128)(2,1)}, bf16[512,2048]{1,0:T(8,128)(2,1)}, bf16[16,2048]{1,0:T(8,128)(2,1)}, bf16[528,256]{1,0:T(8,128)(2,1)}, bf16[528,256]{1,0:T(8,128)(2,1)}) custom-call(bf16[512,2048]{1,0:T(8,128)(2,1)} %x_hbm.1, bf16[512,256]{1,0:T(8,128)(2,1)} %b_hbm.1, bf16[512,256]{1,0:T(8,128)(2,1)} %c_hbm.1, f32[4,2048]{1,0:T(4,128)} %kx.3, ...), custom_call_target="tpu_custom_call" | custom-call | tf_op jit(solution)/shard_map/pallas_call | solution.py:651
  71.7 9.7 %shard_map.130 = (bf16[512,2048]{1,0:T(8,128)(2,1)}, bf16[512,2048]{1,0:T(8,128)(2,1)}, bf16[512,256]{1,0:T(8,128)(2,1)}, bf16[512,256]{1,0:T(8,128)(2,1)}) custom-call(bf16[512,2048]{1,0:T(8,128)(2,1)} %get-tuple-element.9.out, bf16[512,2048]{1,0:T(8,128)(2,1)} %get-tuple-element.10.gp, bf16[16,2048]{1,0:T(8,128)(2,1)} %get-tuple-element.11.gh, ...), custom_call_target="tpu_custom_call" | custom-call | tf_op jit(solution)/shard_map/pallas_call | solution.py:671

commit v3 on v2

--- a/solution.py
+++ b/solution.py
@@ -58,7 +58,7 @@
 def kernel(
     x_hbm, b_hbm, c_hbm, kx, kb, kc, step, dlog, skip, g_hbm,
     out_hbm, gp_hbm, gh_out, gpb_out, gpc_out,
-    xp, bp, cp, gs, cb, lh, cumt, ex, tot, ske,
+    xp, bp, cp, gs, lh, cumt, ex, tot, ske,
     slope, growth, stte, acc_o, acc_g, sx, wx, gw, ls, la,
     gh, gpb, gpc, act_b, act_c, bt, ct, slope_b, slope_c,
     ps, sl, su, grad_b, grad_c,
@@ -121,7 +121,6 @@
         [p.astype(F32) for p in skips] + [zero_s], axis=1
     ).astype(BF)
     ps[...] = jnp.zeros_like(ps)
-    grad_b[...] = jnp.zeros_like(grad_b)
     grad_c[...] = jnp.zeros_like(grad_c)
 
     pl.semaphore_wait(barrier, 8)
@@ -144,6 +143,32 @@
         for ref in (bp, cp, xp):
             ref[head, :] = jnp.zeros((HALO, ref.shape[1]), BF)
 
+    def blk(b):
+        return pl.ds(b * BLOCK, BLOCK)
+
+    def lanes_of(q):
+        return pl.ds(pl.multiple_of(q * W, W), W)
+
+    def spread(q, carry):
+        depth = lax.broadcasted_iota(jnp.int32, (6 * H, 2 * W), 0)
+        col = lax.broadcasted_iota(jnp.int32, (6 * H, 2 * W), 1)
+        hit = (depth % H == 4 * q + (col % W) // 64) & ((depth // (3 * H)) == (col // W))
+        ex[...] = dot(lh[...], hit.astype(F32).astype(BF))
+        ske[q] = ex[pl.ds(T, 8), 0:W]
+        for b in range(NB):
+            cum = ex[blk(b), 0:W]
+            steps = ex[blk(b), W : 2 * W]
+            tot_b = ex[pl.ds(b * BLOCK + BLOCK - 1, 1), 0:W]
+            tot[q, pl.ds(b, 1), :] = tot_b
+            to_end = jnp.exp(tot_b - cum)
+            growth[q, blk(b), :] = jnp.exp(cum)
+            acc_o[q, blk(b), :] = to_end
+            acc_g[q, blk(b), :] = steps
+            stte[q, blk(b), :] = steps * to_end
+        return carry
+
+    lax.fori_loop(0, NQ, spread, 0)
+
     for load in loads:
         load.wait()
 
@@ -153,10 +178,10 @@
             h.wait_recv()
 
     def conv(ref, lanes, taps):
-        cb[...] = ref[:, lanes].astype(F32)
-        pre = taps[0:1] * cb[pl.ds(13, T), :]
-        for k in range(1, 4):
-            pre = pre + taps[k : k + 1] * cb[pl.ds(13 + k, T), :]
+        padded = ref[:, lanes].astype(F32)
+        pre = taps[3:4] * padded[HALO:]
+        for k in range(3):
+            pre = pre + taps[k : k + 1] * pltpu.roll(padded, 3 - k, 0)[HALO:]
         return pre
 
     all_bc = pl.ds(0, ST)
@@ -177,15 +202,10 @@
         sl[b] = scores * lower_f
         su[b] = jnp.transpose(scores) * upper_f
 
-    def blk(b):
-        return pl.ds(b * BLOCK, BLOCK)
-
-    def lanes_of(q):
-        return pl.ds(pl.multiple_of(q * W, W), W)
-
     def order(p):
-        r = (p % 4 + 1) % 4
-        k = p // 4
+        far = p < 6
+        r = jnp.where(far, p % 3 + 1, 0)
+        k = jnp.where(far, p // 3, p - 6)
         return r, k, ((x + r) % 4) * 2 + k
 
     def row_peer(r):
@@ -224,32 +244,18 @@
     def forward_local(p, carry):
         r, k, q = order(p)
         lanes = lanes_of(q)
-        depth = lax.broadcasted_iota(jnp.int32, (6 * H, 2 * W), 0)
-        col = lax.broadcasted_iota(jnp.int32, (6 * H, 2 * W), 1)
-        hit = (depth % H == 4 * q + (col % W) // 64) & ((depth // (3 * H)) == (col // W))
-        ex[...] = dot(lh[...], hit.astype(F32).astype(BF))
-        ske[q] = ex[pl.ds(T, 8), 0:W]
         pre = conv(xp, lanes, kx[:, lanes])
-        sig = sigmoid(pre)
-        slope[q] = sig * (1.0 + pre * (1.0 - sig))
-        act = (pre * sig).astype(BF).astype(F32)
-        cum = ex[pl.ds(0, T), 0:W]
-        steps = ex[pl.ds(0, T), W : 2 * W]
-        acc_o[q] = act * ex[pl.ds(T, 1), 0:W]
-        acc_g[q] = steps
-        growth[q] = jnp.exp(cum)
-        scaled = (act * steps).astype(BF)
+        slope[q] = pre
+        act = (pre * sigmoid(pre)).astype(BF).astype(F32)
+        scaled = (act * acc_g[q]).astype(BF)
         sx[q] = scaled
+        weighted = (scaled.astype(F32) * acc_o[q]).astype(BF)
+        wx[q] = weighted
         state = None
         total = None
         for b in range(NB):
-            tot_b = ex[pl.ds(b * BLOCK + BLOCK - 1, 1), 0:W]
-            tot[q, pl.ds(b, 1), :] = tot_b
-            to_end = jnp.exp(tot_b - ex[blk(b), 0:W])
-            stte[q, blk(b), :] = ex[blk(b), W : 2 * W] * to_end
-            weighted = (scaled[b * BLOCK : (b + 1) * BLOCK].astype(F32) * to_end).astype(BF)
-            wx[q, blk(b), :] = weighted
-            grown = dot(bt[b], weighted)
+            tot_b = tot[q, pl.ds(b, 1), :]
+            grown = dot(bt[b], weighted[b * BLOCK : (b + 1) * BLOCK])
             if b == 0:
                 state, total = grown, tot_b
             else:
@@ -283,7 +289,7 @@
             gw[q, blk(b), :] = grads
             grown = dot(ct[b], grads)
             if b == NB - 1:
-                state = jnp.exp(tot[q, pl.ds(b, 1), :]) * 0.0 + grown
+                state = grown
             else:
                 la[q, b] = state
                 state = jnp.exp(tot[q, pl.ds(b, 1), :]) * state + grown
@@ -329,7 +335,11 @@
                 scaled = sx[q, blk(b), part]
                 grads = gs[blk(b), pl.ds(pl.multiple_of(q * W + pair * BLOCK, BLOCK), BLOCK)]
                 wide_x = halves(scaled)
-                acc_o[q, blk(b), part] += dot(mixing, wide_x)
+                pre = slope[q, blk(b), part]
+                sig = sigmoid(pre)
+                slope[q, blk(b), part] = sig * (1.0 + pre * (1.0 - sig))
+                direct = ske[q, 0:1, part] * (pre * sig).astype(BF).astype(F32)
+                acc_o[q, blk(b), part] = direct + dot(mixing, wide_x)
                 inner = dot(mixing_t, halves(grads))
                 acc_g[q, blk(b), part] = (
                     acc_g[q, blk(b), part] * inner + ske[q, 0:1, part] * grads.astype(F32)
@@ -520,20 +530,21 @@
         gp_copy(q).start()
         return carry
 
-    lax.fori_loop(0, NQ, enter_backward, 0)
-
     for b in range(NB):
         pair_sum = ps[b] * lower_f
         pair_t = jnp.transpose(pair_sum).astype(BF)
-        pair_sum = pair_sum.astype(BF)
-        into_b = grad_b[blk(b), :] + dot(pair_t, act_c[blk(b), :])
-        into_c = grad_c[blk(b), :] + dot(pair_sum, act_b[blk(b), :])
-        gpb[blk(b), :] = (into_b * slope_b[blk(b), :]).astype(BF)
+        grad_b[blk(b), :] = dot(pair_t, act_c[blk(b), :])
+        into_c = grad_c[blk(b), :] + dot(pair_sum.astype(BF), act_b[blk(b), :])
         gpc[blk(b), :] = (into_c * slope_c[blk(b), :]).astype(BF)
+    send_halo(ghalo_c())
+    gpc_out[pl.ds(0, T), :] = gpc[pl.ds(0, T), :]
+
+    lax.fori_loop(0, NQ, enter_backward, 0)
+
+    for b in range(NB):
+        gpb[blk(b), :] = (grad_b[blk(b), :] * slope_b[blk(b), :]).astype(BF)
     send_halo(ghalo_b())
-    send_halo(ghalo_c())
     gpb_out[pl.ds(0, T), :] = gpb[pl.ds(0, T), :]
-    gpc_out[pl.ds(0, T), :] = gpc[pl.ds(0, T), :]
     for q in range(NQ):
         take_halo(ghalo_x(q), gh.at[q])
         gh_out[:, q * W : (q + 1) * W] = gh[q]
@@ -573,23 +584,55 @@
                 yb_cp(r, k).wait_send()
 
 
-def back_kernel(out, gp, gh, gpb, gpc, kx, kb, kc, out_ref, gx_ref, gb_ref, gc_ref, cb):
-    def back(taps):
-        grad = taps[0:1] * cb[pl.ds(3, T), :]
-        for k in range(1, 4):
-            grad = grad + taps[k : k + 1] * cb[pl.ds(3 - k, T), :]
+def back_kernel(
+    out_hbm, gp_hbm, gh_hbm, gpb, gpc, kx, kb, kc, out_ref, gx_ref, gb_ref, gc_ref,
+    out_v, gp_v, gx_v, in_sem, out_sem,
+):
+    def rows(i):
+        return pl.ds(i * BLOCK, BLOCK)
+
+    loads = [pltpu.make_async_copy(gh_hbm, gp_v.at[pl.ds(T, HALO)], in_sem.at[2 * NB])]
+    for i in reversed(range(NB)):
+        loads.append(pltpu.make_async_copy(gp_hbm.at[rows(i)], gp_v.at[rows(i)], in_sem.at[i]))
+    passed = [
+        pltpu.make_async_copy(out_hbm.at[rows(i)], out_v.at[rows(i)], in_sem.at[NB + i])
+        for i in range(NB)
+    ]
+    for copy in loads + passed:
+        copy.start()
+
+    def back(value, taps, count):
+        value = value.astype(F32)
+        size = value.shape[0]
+        grad = taps[3:4] * value[:count]
+        for k in range(3):
+            grad = grad + taps[k : k + 1] * pltpu.roll(value, size - (3 - k), 0)[:count]
         return grad.astype(BF)
 
-    out_ref[...] = out[...]
-    cb[pl.ds(0, T), :] = gp[...].astype(F32)
-    cb[pl.ds(T, HALO), :] = gh[...].astype(F32)
-    gx_ref[...] = back(kx[...])
-
-    @pl.when(pl.program_id(0) == 0)
-    def _():
-        for ref, taps, res in ((gpb, kb, gb_ref), (gpc, kc, gc_ref)):
-            cb[...] = ref[...].astype(F32)
-            res[...] = back(taps[...])
+    gb_ref[...] = back(gpb[...], kb[...], T)
+    gc_ref[...] = back(gpc[...], kc[...], T)
+    stores = []
+    loads[0].wait()
+    for i in reversed(range(NB)):
+        loads[NB - i].wait()
+
+        def slab(q, carry):
+            lanes = pl.ds(pl.multiple_of(q * W, W), W)
+            value = gp_v[pl.ds(i * BLOCK, BLOCK + HALO), lanes]
+            gx_v[rows(i), lanes] = back(value, kx[:, lanes], BLOCK)
+            return carry
+
+        lax.fori_loop(0, NQ, slab, 0)
+        stores.append(pltpu.make_async_copy(gx_v.at[rows(i)], gx_ref.at[rows(i)], out_sem.at[i]))
+        stores[-1].start()
+    for i in range(NB):
+        passed[i].wait()
+        stores.append(
+            pltpu.make_async_copy(out_v.at[rows(i)], out_ref.at[rows(i)], out_sem.at[NB + i])
+        )
+        stores[-1].start()
+    for copy in stores:
+        copy.wait()
 
 
 def on_device(x, b, c, kx, kb, kc, step, dlog, skip, g):
@@ -602,7 +645,6 @@
         pltpu.VMEM((T + HALO, ST), BF),
         pltpu.VMEM((T + HALO, ST), BF),
         pltpu.VMEM((T, NQ * W), BF),
-        pltpu.VMEM((T + HALO, W), F32),
         pltpu.VMEM((T + 16, 6 * H), BF),
         pltpu.VMEM((NQ, 8, T), F32),
         pltpu.VMEM((T + 16, 2 * W), F32),
@@ -664,25 +706,23 @@
             collective_id=0, has_side_effects=True, vmem_limit_bytes=67043328
         ),
     )(x, b, c, kx, kb, kc, step.T, dlog.reshape(1, H), skip.reshape(1, H), g)
-    slab = pl.BlockSpec((T, W), lambda q: (0, q))
-    whole = pl.BlockSpec((T, ST), lambda q: (0, 0))
-    padded = pl.BlockSpec((T + HALO, ST), lambda q: (0, 0))
-    small = pl.BlockSpec((4, ST), lambda q: (0, 0))
     return pl.pallas_call(
         back_kernel,
-        grid=(NQ,),
         out_shape=(
             jax.ShapeDtypeStruct(x.shape, BF),
             jax.ShapeDtypeStruct(x.shape, BF),
             jax.ShapeDtypeStruct(b.shape, BF),
             jax.ShapeDtypeStruct(c.shape, BF),
         ),
-        in_specs=[
-            slab, slab, pl.BlockSpec((HALO, W), lambda q: (0, q)), padded, padded,
-            pl.BlockSpec((4, W), lambda q: (0, q)), small, small,
+        in_specs=[hbm] * 3 + [vmem] * 5,
+        out_specs=(hbm, hbm, vmem, vmem),
+        scratch_shapes=[
+            pltpu.VMEM((T, NQ * W), BF),
+            pltpu.VMEM((T + HALO, NQ * W), BF),
+            pltpu.VMEM((T, NQ * W), BF),
+            dma((2 * NB + 1,)),
+            dma((2 * NB,)),
         ],
-        out_specs=(slab, slab, whole, whole),
-        scratch_shapes=[pltpu.VMEM((T + HALO, W), F32)],
     )(out, gp, gh, gpb, gpc, kx, kb, kc)
 
 

time: 81.8 us -> 74.4 us (0.910)
  Pallas kernels: 80.8 us -> 73.5 us
    pallas_call x1, Pallas kernels: 71.1 us -> 66.8 us  [on_device(): pl.pallas_call(kernel, out_shape=(jax.ShapeDtypeStruct(x.shape, BF), jax....]
    pallas_call x1, Pallas kernels: 9.74 us -> 6.78 us  [on_device(): pl.pallas_call(back_kernel, out_shape=(jax.ShapeDtypeStruct(x.shape, BF),...]
where the time goes in v3:
time: 74.4 us; the launch traced here: 74.2 us
  Pallas kernels  73.5 us (99%)
    pallas_call x1, Pallas kernels, on_device(): pl.pallas_call(kernel, out_shape=(jax.ShapeDtypeStruct(x.shape, BF), jax....  66.8 us
    pallas_call x1, Pallas kernels, on_device(): pl.pallas_call(back_kernel, out_shape=(jax.ShapeDtypeStruct(x.shape, BF),...  6.78 us

profile of v3, /device:TPU:2, one launch (start us, length us, event | category | flops | bytes accessed | tf_op | source)
XLA Modules:
  0.0 74.2 jit_solution(5030677679222562847)
XLA Ops:
  0.6 66.8 %shard_map.129 = (bf16[512,2048]{1,0:T(8,128)(2,1)}, bf16[512,2048]{1,0:T(8,128)(2,1)}, bf16[16,2048]{1,0:T(8,128)(2,1)}, bf16[528,256]{1,0:T(8,128)(2,1)}, bf16[528,256]{1,0:T(8,128)(2,1)}) custom-call(bf16[512,2048]{1,0:T(8,128)(2,1)} %x_hbm.1, bf16[512,256]{1,0:T(8,128)(2,1)} %b_hbm.1, bf16[512,256]{1,0:T(8,128)(2,1)} %c_hbm.1, f32[4,2048]{1,0:T(4,128)} %kx.3, ...), custom_call_target="tpu_custom_call" | custom-call | tf_op jit(solution)/shard_map/pallas_call | solution.py:693
  67.4 6.8 %shard_map.130 = (bf16[512,2048]{1,0:T(8,128)(2,1)}, bf16[512,2048]{1,0:T(8,128)(2,1)}, bf16[512,256]{1,0:T(8,128)(2,1)}, bf16[512,256]{1,0:T(8,128)(2,1)}) custom-call(bf16[512,2048]{1,0:T(8,128)(2,1)} %get-tuple-element.9.out_hbm, bf16[512,2048]{1,0:T(8,128)(2,1)} %get-tuple-element.10.gp_hbm, bf16[16,2048]{1,0:T(8,128)(2,1)} %get-tuple-element.11.gh_hbm, ...), custom_call_target="tpu_custom_call" | custom-call | tf_op jit(solution)/shard_map/pallas_call | solution.py:709

commit v4 on v3

--- a/solution.py
+++ b/solution.py
@@ -184,23 +184,16 @@
             pre = pre + taps[k : k + 1] * pltpu.roll(padded, 3 - k, 0)[HALO:]
         return pre
 
-    all_bc = pl.ds(0, ST)
-    for ref, taps, act, act_t, slo in (
-        (bp, kb, act_b, bt, slope_b),
-        (cp, kc, act_c, ct, slope_c),
-    ):
-        pre = conv(ref, all_bc, taps[...])
+    def prepare(ref, taps, act, act_t, slo):
+        pre = conv(ref, pl.ds(0, ST), taps[...])
         sig = sigmoid(pre)
         slo[...] = sig * (1.0 + pre * (1.0 - sig))
         value = (pre * sig).astype(BF)
         act[...] = value
         for b in range(NB):
             act_t[b] = jnp.transpose(value[b * BLOCK : (b + 1) * BLOCK].astype(F32)).astype(BF)
-    for b in range(NB):
-        rows = pl.ds(b * BLOCK, BLOCK)
-        scores = dot_nt(act_c[rows, :], act_b[rows, :])
-        sl[b] = scores * lower_f
-        su[b] = jnp.transpose(scores) * upper_f
+
+    prepare(bp, kb, act_b, bt, slope_b)
 
     def order(p):
         far = p < 6
@@ -280,6 +273,8 @@
 
     lax.fori_loop(0, NQ, forward_local, 0)
 
+    prepare(cp, kc, act_c, ct, slope_c)
+
     def backward_local(p, carry):
         r, k, q = order(p)
         lanes = lanes_of(q)
@@ -307,6 +302,11 @@
         return carry
 
     lax.fori_loop(0, NQ, backward_local, 0)
+
+    for b in range(NB):
+        scores = dot_nt(act_c[blk(b), :], act_b[blk(b), :])
+        sl[b] = scores * lower_f
+        su[b] = jnp.transpose(scores) * upper_f
 
     left = lax.broadcasted_iota(jnp.int32, (BLOCK, BLOCK), 1) < 64
 
@@ -428,21 +428,15 @@
         for r in range(1, 4):
             b2(r, k).start()
 
-    lax.fori_loop(0, 3, intra, 0)
-    for k in range(2):
+    def take_forward(k):
         for r in range(1, 4):
             f1(r, k).wait_recv()
         row_forward(k)
-    lax.fori_loop(3, 7, intra, 0)
-    for k in range(2):
-        finish_forward(k)
-    for k in range(2):
+
+    def take_backward(k):
         for r in range(1, 4):
             b1(r, k).wait_recv()
         row_backward(k)
-    lax.fori_loop(7, 8, intra, 0)
-    for k in range(2):
-        finish_backward(k)
 
     def order_in(p):
         r = p % 4
@@ -477,7 +471,20 @@
         out_copy(q).start()
         return carry
 
-    lax.fori_loop(0, NQ, enter_forward, 0)
+    take_forward(0)
+    lax.fori_loop(0, 3, intra, 0)
+    take_forward(1)
+    lax.fori_loop(3, 6, intra, 0)
+    finish_forward(0)
+    take_backward(0)
+    lax.fori_loop(6, 7, intra, 0)
+    finish_forward(1)
+    take_backward(1)
+    lax.fori_loop(7, NQ, intra, 0)
+    finish_backward(0)
+    lax.fori_loop(0, 4, enter_forward, 0)
+    finish_backward(1)
+    lax.fori_loop(4, NQ, enter_forward, 0)
 
     tail = pl.ds(T, HALO)
 

time: 74.4 us -> 71 us (0.954)
  Pallas kernels: 73.5 us -> 70.1 us
    pallas_call x1, Pallas kernels: 66.8 us -> 63.4 us  [on_device(): pl.pallas_call(kernel, out_shape=(jax.ShapeDtypeStruct(x.shape, BF), jax....]
where the time goes in v4:
time: 71 us; the launch traced here: 70.8 us
  Pallas kernels  70.1 us (99%)
    pallas_call x1, Pallas kernels, on_device(): pl.pallas_call(kernel, out_shape=(jax.ShapeDtypeStruct(x.shape, BF), jax....  63.4 us
    pallas_call x1, Pallas kernels, on_device(): pl.pallas_call(back_kernel, out_shape=(jax.ShapeDtypeStruct(x.shape, BF),...  6.78 us

profile of v4, /device:TPU:2, one launch (start us, length us, event | category | flops | bytes accessed | tf_op | source)
XLA Modules:
  0.0 70.8 jit_solution(10968922878258163792)
XLA Ops:
  0.6 63.4 %shard_map.129 = (bf16[512,2048]{1,0:T(8,128)(2,1)}, bf16[512,2048]{1,0:T(8,128)(2,1)}, bf16[16,2048]{1,0:T(8,128)(2,1)}, bf16[528,256]{1,0:T(8,128)(2,1)}, bf16[528,256]{1,0:T(8,128)(2,1)}) custom-call(bf16[512,2048]{1,0:T(8,128)(2,1)} %x_hbm.1, bf16[512,256]{1,0:T(8,128)(2,1)} %b_hbm.1, bf16[512,256]{1,0:T(8,128)(2,1)} %c_hbm.1, f32[4,2048]{1,0:T(4,128)} %kx.3, ...), custom_call_target="tpu_custom_call" | custom-call | tf_op jit(solution)/shard_map/pallas_call | solution.py:700
  64.0 6.8 %shard_map.130 = (bf16[512,2048]{1,0:T(8,128)(2,1)}, bf16[512,2048]{1,0:T(8,128)(2,1)}, bf16[512,256]{1,0:T(8,128)(2,1)}, bf16[512,256]{1,0:T(8,128)(2,1)}) custom-call(bf16[512,2048]{1,0:T(8,128)(2,1)} %get-tuple-element.9.out_hbm, bf16[512,2048]{1,0:T(8,128)(2,1)} %get-tuple-element.10.gp_hbm, bf16[16,2048]{1,0:T(8,128)(2,1)} %get-tuple-element.11.gh_hbm, ...), custom_call_target="tpu_custom_call" | custom-call | tf_op jit(solution)/shard_map/pallas_call | solution.py:716

commit v5 on v4

--- a/solution.py
+++ b/solution.py
@@ -149,7 +149,14 @@
     def lanes_of(q):
         return pl.ds(pl.multiple_of(q * W, W), W)
 
-    def spread(q, carry):
+    def order(p):
+        far = p < 6
+        r = jnp.where(far, jnp.where(p % 3 == 0, 2, jnp.where(p % 3 == 1, 1, 3)), 0)
+        k = jnp.where(far, p // 3, p - 6)
+        return r, k, ((x + r) % 4) * 2 + k
+
+    def spread(p, carry):
+        q = order(p)[2]
         depth = lax.broadcasted_iota(jnp.int32, (6 * H, 2 * W), 0)
         col = lax.broadcasted_iota(jnp.int32, (6 * H, 2 * W), 1)
         hit = (depth % H == 4 * q + (col % W) // 64) & ((depth // (3 * H)) == (col // W))
@@ -167,7 +174,7 @@
             stte[q, blk(b), :] = steps * to_end
         return carry
 
-    lax.fori_loop(0, NQ, spread, 0)
+    lax.fori_loop(0, 3, spread, 0)
 
     for load in loads:
         load.wait()
@@ -194,12 +201,6 @@
             act_t[b] = jnp.transpose(value[b * BLOCK : (b + 1) * BLOCK].astype(F32)).astype(BF)
 
     prepare(bp, kb, act_b, bt, slope_b)
-
-    def order(p):
-        far = p < 6
-        r = jnp.where(far, p % 3 + 1, 0)
-        k = jnp.where(far, p // 3, p - 6)
-        return r, k, ((x + r) % 4) * 2 + k
 
     def row_peer(r):
         return y * 4 + (x + r) % 4
@@ -271,7 +272,9 @@
 
         return carry
 
-    lax.fori_loop(0, NQ, forward_local, 0)
+    lax.fori_loop(0, 3, forward_local, 0)
+    lax.fori_loop(3, NQ, spread, 0)
+    lax.fori_loop(3, NQ, forward_local, 0)
 
     prepare(cp, kc, act_c, ct, slope_c)
 
@@ -592,8 +595,8 @@
 
 
 def back_kernel(
-    out_hbm, gp_hbm, gh_hbm, gpb, gpc, kx, kb, kc, out_ref, gx_ref, gb_ref, gc_ref,
-    out_v, gp_v, gx_v, in_sem, out_sem,
+    out_hbm, gp_hbm, gh_hbm, gpb_hbm, gpc_hbm, kx, kb, kc, out_ref, gx_ref, gb_ref, gc_ref,
+    out_v, gp_v, gx_v, gpb, gpc, gb_v, gc_v, in_sem, out_sem,
 ):
     def rows(i):
         return pl.ds(i * BLOCK, BLOCK)
@@ -601,6 +604,8 @@
     loads = [pltpu.make_async_copy(gh_hbm, gp_v.at[pl.ds(T, HALO)], in_sem.at[2 * NB])]
     for i in reversed(range(NB)):
         loads.append(pltpu.make_async_copy(gp_hbm.at[rows(i)], gp_v.at[rows(i)], in_sem.at[i]))
+    loads.append(pltpu.make_async_copy(gpb_hbm, gpb, in_sem.at[2 * NB + 1]))
+    loads.append(pltpu.make_async_copy(gpc_hbm, gpc, in_sem.at[2 * NB + 2]))
     passed = [
         pltpu.make_async_copy(out_hbm.at[rows(i)], out_v.at[rows(i)], in_sem.at[NB + i])
         for i in range(NB)
@@ -616,9 +621,12 @@
             grad = grad + taps[k : k + 1] * pltpu.roll(value, size - (3 - k), 0)[:count]
         return grad.astype(BF)
 
-    gb_ref[...] = back(gpb[...], kb[...], T)
-    gc_ref[...] = back(gpc[...], kc[...], T)
     stores = []
+
+    def store(src, dst, slot):
+        stores.append(pltpu.make_async_copy(src, dst, out_sem.at[slot]))
+        stores[-1].start()
+
     loads[0].wait()
     for i in reversed(range(NB)):
         loads[NB - i].wait()
@@ -630,14 +638,17 @@
             return carry
 
         lax.fori_loop(0, NQ, slab, 0)
-        stores.append(pltpu.make_async_copy(gx_v.at[rows(i)], gx_ref.at[rows(i)], out_sem.at[i]))
-        stores[-1].start()
-    for i in range(NB):
-        passed[i].wait()
-        stores.append(
-            pltpu.make_async_copy(out_v.at[rows(i)], out_ref.at[rows(i)], out_sem.at[NB + i])
-        )
-        stores[-1].start()
+        store(gx_v.at[rows(i)], gx_ref.at[rows(i)], i)
+        if i % 2 == 1:
+            for j in (i - 1, i):
+                passed[j].wait()
+                store(out_v.at[rows(j)], out_ref.at[rows(j)], NB + j)
+    loads[NB + 1].wait()
+    gb_v[...] = back(gpb[...], kb[...], T)
+    store(gb_v, gb_ref, 2 * NB)
+    loads[NB + 2].wait()
+    gc_v[...] = back(gpc[...], kc[...], T)
+    store(gc_v, gc_ref, 2 * NB + 1)
     for copy in stores:
         copy.wait()
 
@@ -721,14 +732,18 @@
             jax.ShapeDtypeStruct(b.shape, BF),
             jax.ShapeDtypeStruct(c.shape, BF),
         ),
-        in_specs=[hbm] * 3 + [vmem] * 5,
-        out_specs=(hbm, hbm, vmem, vmem),
+        in_specs=[hbm] * 5 + [vmem] * 3,
+        out_specs=(hbm,) * 4,
         scratch_shapes=[
             pltpu.VMEM((T, NQ * W), BF),
             pltpu.VMEM((T + HALO, NQ * W), BF),
             pltpu.VMEM((T, NQ * W), BF),
-            dma((2 * NB + 1,)),
-            dma((2 * NB,)),
+            pltpu.VMEM((T + HALO, ST), BF),
+            pltpu.VMEM((T + HALO, ST), BF),
+            pltpu.VMEM((T, ST), BF),
+            pltpu.VMEM((T, ST), BF),
+            dma((2 * NB + 3,)),
+            dma((2 * NB + 2,)),
         ],
     )(out, gp, gh, gpb, gpc, kx, kb, kc)
 

time: 71 us -> 69.9 us (0.985); the launches traced: 70.8 us -> 68.8 us
  Pallas kernels: 70.1 us -> 68.2 us
    pallas_call x1, Pallas kernels: 63.4 us -> 62 us  [on_device(): pl.pallas_call(kernel, out_shape=(jax.ShapeDtypeStruct(x.shape, BF), jax....]
where the time goes in v5:
time: 69.9 us; the launch traced here: 68.8 us
  Pallas kernels  68.2 us (98%)
    pallas_call x1, Pallas kernels, on_device(): pl.pallas_call(kernel, out_shape=(jax.ShapeDtypeStruct(x.shape, BF), jax....  62 us
    pallas_call x1, Pallas kernels, on_device(): pl.pallas_call(back_kernel, out_shape=(jax.ShapeDtypeStruct(x.shape, BF),...  6.18 us

profile of v5, /device:TPU:2, one launch (start us, length us, event | category | flops | bytes accessed | tf_op | source)
XLA Modules:
  0.0 68.8 jit_solution(10562662248760415112)
XLA Ops:
  0.6 62.0 %shard_map.129 = (bf16[512,2048]{1,0:T(8,128)(2,1)}, bf16[512,2048]{1,0:T(8,128)(2,1)}, bf16[16,2048]{1,0:T(8,128)(2,1)}, bf16[528,256]{1,0:T(8,128)(2,1)}, bf16[528,256]{1,0:T(8,128)(2,1)}) custom-call(bf16[512,2048]{1,0:T(8,128)(2,1)} %x_hbm.1, bf16[512,256]{1,0:T(8,128)(2,1)} %b_hbm.1, bf16[512,256]{1,0:T(8,128)(2,1)} %c_hbm.1, f32[4,2048]{1,0:T(4,128)} %kx.3, ...), custom_call_target="tpu_custom_call" | custom-call | tf_op jit(solution)/shard_map/pallas_call | solution.py:711
  62.6 6.2 %shard_map.130 = (bf16[512,2048]{1,0:T(8,128)(2,1)}, bf16[512,2048]{1,0:T(8,128)(2,1)}, bf16[512,256]{1,0:T(8,128)(2,1)}, bf16[512,256]{1,0:T(8,128)(2,1)}) custom-call(bf16[512,2048]{1,0:T(8,128)(2,1)} %get-tuple-element.9.out_hbm, bf16[512,2048]{1,0:T(8,128)(2,1)} %get-tuple-element.10.gp_hbm, bf16[16,2048]{1,0:T(8,128)(2,1)} %get-tuple-element.11.gh_hbm, ...), custom_call_target="tpu_custom_call" | custom-call | tf_op jit(solution)/shard_map/pallas_call | solution.py:727

commit v6 on v5

--- a/solution.py
+++ b/solution.py
@@ -524,19 +524,22 @@
         def _():
             b2(r, k).wait_recv()
 
-        after = inb[q]
-        base = after.astype(F32)
-        total = None
-        for b in reversed(range(NB)):
+        base = inb[q].astype(F32)
+        totals = [None] * NB
+        for b in reversed(range(NB - 1)):
+            tot_b = tot[q, pl.ds(b + 1, 1), :]
+            totals[b] = tot_b if b == NB - 2 else totals[b + 1] + tot_b
+        for b in range(NB):
             if b < NB - 1:
-                tot_b = tot[q, pl.ds(b + 1, 1), :]
-                total = tot_b if b == NB - 2 else total + tot_b
-                after = (la[q, b] + jnp.exp(total) * base).astype(BF)
+                after = (la[q, b] + jnp.exp(totals[b]) * base).astype(BF)
+            else:
+                after = inb[q]
             outer = stte[q, blk(b), :] * dot(act_b[blk(b), :], after)
             grads = (acc_g[q, blk(b), :] + outer) * slope[q, blk(b), :]
             gs[blk(b), lanes_of(q)] = grads.astype(BF)
+            if b == 0:
+                send_halo(ghalo_x(q))
             grad_b[blk(b), :] += dot_nt(wx[q, blk(b), :], after)
-        send_halo(ghalo_x(q))
         gp_copy(q).start()
         return carry
 
@@ -551,9 +554,10 @@
 
     lax.fori_loop(0, NQ, enter_backward, 0)
 
-    for b in range(NB):
+    gpb[blk(0), :] = (grad_b[blk(0), :] * slope_b[blk(0), :]).astype(BF)
+    send_halo(ghalo_b())
+    for b in range(1, NB):
         gpb[blk(b), :] = (grad_b[blk(b), :] * slope_b[blk(b), :]).astype(BF)
-    send_halo(ghalo_b())
     gpb_out[pl.ds(0, T), :] = gpb[pl.ds(0, T), :]
     for q in range(NQ):
         take_halo(ghalo_x(q), gh.at[q])

time: 69.9 us -> 70.1 us (level)
  no operation moved by 1% of the time
where the time goes in v6:
time: 70.1 us; the launch traced here: 68.9 us
  Pallas kernels  68.2 us (97%)
    pallas_call x1, Pallas kernels, on_device(): pl.pallas_call(kernel, out_shape=(jax.ShapeDtypeStruct(x.shape, BF), jax....  62.1 us
    pallas_call x1, Pallas kernels, on_device(): pl.pallas_call(back_kernel, out_shape=(jax.ShapeDtypeStruct(x.shape, BF),...  6.18 us

profile of v6, /device:TPU:2, one launch (start us, length us, event | category | flops | bytes accessed | tf_op | source)
XLA Modules:
  0.0 68.9 jit_solution(16058106491798077192)
XLA Ops:
  0.6 62.1 %shard_map.129 = (bf16[512,2048]{1,0:T(8,128)(2,1)}, bf16[512,2048]{1,0:T(8,128)(2,1)}, bf16[16,2048]{1,0:T(8,128)(2,1)}, bf16[528,256]{1,0:T(8,128)(2,1)}, bf16[528,256]{1,0:T(8,128)(2,1)}) custom-call(bf16[512,2048]{1,0:T(8,128)(2,1)} %x_hbm.1, bf16[512,256]{1,0:T(8,128)(2,1)} %b_hbm.1, bf16[512,256]{1,0:T(8,128)(2,1)} %c_hbm.1, f32[4,2048]{1,0:T(4,128)} %kx.3, ...), custom_call_target="tpu_custom_call" | custom-call | tf_op jit(solution)/shard_map/pallas_call | solution.py:715
  62.7 6.2 %shard_map.130 = (bf16[512,2048]{1,0:T(8,128)(2,1)}, bf16[512,2048]{1,0:T(8,128)(2,1)}, bf16[512,256]{1,0:T(8,128)(2,1)}, bf16[512,256]{1,0:T(8,128)(2,1)}) custom-call(bf16[512,2048]{1,0:T(8,128)(2,1)} %get-tuple-element.9.out_hbm, bf16[512,2048]{1,0:T(8,128)(2,1)} %get-tuple-element.10.gp_hbm, bf16[16,2048]{1,0:T(8,128)(2,1)} %get-tuple-element.11.gh_hbm, ...), custom_call_target="tpu_custom_call" | custom-call | tf_op jit(solution)/shard_map/pallas_call | solution.py:731
